TPU v7x, 128 devices: a whole 4x4x4 slice. The times are simulated.
128 devices in a mesh: span: 16 (over x, z), chord: 8 (over y, core).
Axes of the slice: x: 4, y: 4, z: 4, core: 2. Of those that a mesh axis runs over, the one named last changes fastest.
Arguments:
- fluid_state: float32 [4, 512, 256, 128], P(None, 'span', 'chord'), may hold values from -6 to 6
- shell_disp: float32 [3, 2048, 1024], P(None, 'span', 'chord'), may hold values from -6 to 6
- shell_vel: float32 [3, 2048, 1024], P(None, 'span', 'chord'), may hold values from -6 to 6
- owners: int32 [131072, 4], P(('span', 'chord')), may hold values from 0 to 127, all different within a row; in each aligned block of 1024 rows (0 to 1023, 1024 to 2047, ...) at most 64 rows name the same one
- node_local: int32 [131072, 4], P(('span', 'chord')), may hold values from 0 to 16383
- rbf_weight: float32 [131072, 4], P(('span', 'chord')), may hold values from 0.2 to 1
- normals: float32 [3, 131072], P(None, ('span', 'chord')), may hold values from -6 to 6
Outputs:
- fluid_next: float32 [4, 512, 256, 128], P(None, 'span', 'chord')
- interface_motion: float32 [6, 131072], P(None, ('span', 'chord'))
- disp_next: float32 [3, 2048, 1024], P(None, 'span', 'chord')
- vel_next: float32 [3, 2048, 1024], P(None, 'span', 'chord')
Inputs may be any that keep to these rules, and one draw needn't show every extreme that they name: Each interface point names 4 different owners; the points of one device name no owner more than 64 times, a bound that some block reaches.
All inputs are finite; a program needn't handle non-finite values.
Results may differ from a plain program's by a relative error of at most 0.00007.
Values sent between devices are 32-bit elements; how exact they have to be, the bound alone decides.
A program may use at most 64 MiB of HBM per device.

v0:
```python
import jax
import jax.numpy as jnp
from jax import lax
from jax.sharding import PartitionSpec as P

flow_speed = 0.5
time_step = 0.4
stiffness = 0.5
damping = 0.2
shell_step = 0.3


def with_halo(value, sides, width):
    edges = {}
    for axis, dim in sides:
        size, length = (lax.axis_size(axis), value.shape[dim])
        up = [(i, (i + 1) % size) for i in range(size - 1)]
        last = lax.slice_in_dim(value, length - width, length, axis=dim)
        leading = lax.slice_in_dim(value, 0, width, axis=dim)
        edges[dim] = (
            lax.ppermute(last, axis, up),
            lax.ppermute(leading, axis, [(b, a) for a, b in up]),
        )
    done = []
    for _, dim in sides:
        low, high = edges[dim]
        around = [(width, width) if d in done else (0, 0) for d in range(value.ndim)]
        value = jnp.concatenate([jnp.pad(low, around), value, jnp.pad(high, around)], axis=dim)
        done.append(dim)
    return value


def central(padded, direction):
    length = padded.shape[direction] - 6

    def window(offset):
        return lax.slice_in_dim(padded, 3 + offset, 3 + offset + length, axis=direction)

    return (
        45.0 * (window(1) - window(-1)) - 9.0 * (window(2) - window(-2)) + (window(3) - window(-3))
    ) / 60.0


def stencil_coef(distance):
    size = jnp.abs(distance)
    value = jnp.where(size == 1, 45.0, jnp.where(size == 2, -9.0, jnp.where(size == 3, 1.0, 0.0)))
    return value * jnp.sign(distance).astype(jnp.float32) / 60.0


def normal_tables(length):
    source = lax.broadcasted_iota(jnp.int32, (length, length), 0)
    target = lax.broadcasted_iota(jnp.int32, (length, length), 1)
    inner = stencil_coef(source - target)
    ghost = jnp.where(source < 3, stencil_coef(-(source + 1 + target)), 0.0)
    pressure_table = inner + ghost
    normal_table = inner - ghost
    wall_row = 2.0 * jnp.sum(ghost, axis=0)
    return (pressure_table, normal_table, wall_row)


def normal_derivatives(fluid, wall_motion):
    cells_x, cells_y, length = (fluid.shape[1], fluid.shape[2], fluid.shape[3])
    pressure_table, normal_table, wall_row = normal_tables(length)
    pressure_flat = fluid[0].reshape(cells_x * cells_y, length)
    normal_flat = fluid[3].reshape(cells_x * cells_y, length)
    dz_pressure = jnp.dot(
        pressure_flat,
        pressure_table,
        precision=lax.Precision.HIGHEST,
        preferred_element_type=jnp.float32,
    )
    dz_normal = jnp.dot(
        normal_flat,
        normal_table,
        precision=lax.Precision.HIGHEST,
        preferred_element_type=jnp.float32,
    )
    dz_normal = dz_normal + wall_motion[2].reshape(-1)[:, None] * wall_row[None, :]
    return (
        dz_pressure.reshape(cells_x, cells_y, length),
        dz_normal.reshape(cells_x, cells_y, length),
    )


def fluid_rates(span_padded, chord_padded, dz_pressure, dz_normal):
    along_span = central(span_padded, 1)
    along_chord = central(chord_padded, 2)
    rate_p = -flow_speed * along_span[0] - (along_span[1] + along_chord[1] + dz_normal)
    rate_u = -flow_speed * along_span[1] - along_span[0]
    rate_v = -flow_speed * along_span[2] - along_chord[0]
    rate_w = -flow_speed * along_span[3] - dz_pressure
    return jnp.stack([rate_p, rate_u, rate_v, rate_w])


def laplacian(padded):
    center = padded[:, 1:-1, 1:-1]
    return (
        padded[:, 2:, 1:-1]
        + padded[:, :-2, 1:-1]
        + padded[:, 1:-1, 2:]
        + padded[:, 1:-1, :-2]
        - 4.0 * center
    )


def body(fluid_state, shell_disp, shell_vel, owners, node_local, rbf_weight, normals):
    span_count = lax.axis_size("span")
    chord_count = lax.axis_size("chord")
    devices = span_count * chord_count
    points, stencil = owners.shape
    capacity = max(2, (2 * points * stencil + devices - 1) // devices)
    owner_ids = owners.reshape(-1)
    node_ids = node_local.reshape(-1)
    columns = jnp.arange(devices, dtype=jnp.int32)
    onehot = (owner_ids[:, None] == columns[None, :]).astype(jnp.int32)
    before = jnp.cumsum(onehot, axis=0) - onehot
    order_in = jnp.sum(before * onehot, axis=1)
    slot_index = owner_ids * capacity + order_in
    requests = jnp.zeros((devices * capacity,), jnp.int32).at[slot_index].set(node_ids)
    asked_nodes = lax.all_to_all(
        requests, ("span", "chord"), split_axis=0, concat_axis=0, tiled=True
    )
    rows_x, rows_y = (shell_disp.shape[1], shell_disp.shape[2])
    stacked = jnp.concatenate([shell_disp, shell_vel], axis=0).reshape(6, rows_x * rows_y)
    picked = jnp.take(stacked, asked_nodes, axis=1)
    replies = lax.all_to_all(picked, ("span", "chord"), split_axis=1, concat_axis=1, tiled=True)
    motion = jnp.take(replies, slot_index, axis=1).reshape(6, points, stencil)
    interface_motion = jnp.sum(motion * rbf_weight[None], axis=2)
    cells_x, cells_y = (fluid_state.shape[1], fluid_state.shape[2])
    wall_motion = interface_motion[3:].reshape(3, cells_x, cells_y)
    padded_all = with_halo(fluid_state, (("span", 1), ("chord", 2)), 3)
    span_padded = padded_all[:, :, 3:-3]
    chord_padded = padded_all[0::2, 3:-3]
    dz_pressure, dz_normal = normal_derivatives(fluid_state, wall_motion)
    fluid_next = fluid_state + time_step * fluid_rates(
        span_padded, chord_padded, dz_pressure, dz_normal
    )
    pressure = fluid_next[0, :, :, 0].reshape(-1)
    surface_load = normals * pressure[None]
    contrib = (surface_load[:, :, None] * rbf_weight[None]).reshape(3, -1)
    outgoing = jnp.zeros((3, devices * capacity), jnp.float32).at[:, slot_index].set(contrib)
    arrived = lax.all_to_all(outgoing, ("span", "chord"), split_axis=1, concat_axis=1, tiled=True)
    shell_force = (
        jnp.zeros((3, rows_x * rows_y), jnp.float32)
        .at[:, asked_nodes]
        .add(arrived)
        .reshape(3, rows_x, rows_y)
    )
    shell_padded = with_halo(shell_disp, (("span", 1), ("chord", 2)), 1)
    bending = laplacian(shell_padded)
    acceleration = stiffness * bending + shell_force - damping * shell_vel
    vel_next = shell_vel + shell_step * acceleration
    disp_next = shell_disp + shell_step * vel_next
    return (fluid_next, interface_motion, disp_next, vel_next)


def solution(mesh):
    placed = (
        P(None, "span", "chord", None),
        P(None, "span", "chord"),
        P(None, "span", "chord"),
        P(("span", "chord"), None),
        P(("span", "chord"), None),
        P(("span", "chord"), None),
        P(None, ("span", "chord")),
    )
    return jax.shard_map(
        body,
        mesh=mesh,
        in_specs=placed,
        out_specs=(
            P(None, "span", "chord", None),
            P(None, ("span", "chord")),
            P(None, "span", "chord"),
            P(None, "span", "chord"),
        ),
        check_vma=False,
    )
```

profile of v0, /device:TPU:17, one launch (start us, length us, event | category | flops | bytes accessed | tf_op | source)
XLA Modules:
  0.0 271.4 jit_solution(8638491688698417619)
XLA Ops:
  0.6 0.7 broadcast_multiply_fusion.1
  1.4 0.9 copy.89
  3.5 0.6 fusion.14
  4.4 2.5 copy.92
  7.5 2.6 fusion.9
  10.2 15.5 %scatter_custom_fusion = s32[8192]{0:T(1024)S(1)} fusion(s32[4096]{0:T(1024)S(1)} %bitcast.66, s32[4096]{0:T(1024)S(1)} %reshape.173, s32[]{:T(128)} %constant.34.clone.1), kind=kCustom, calls=%fused_computation.124 | custom fusion | bytes 32772 | tf_op jit(solution)/shard_map/scatter | solution.py:119
  25.7 0.7 all_to_all.24
  26.4 11.1 %all-to-all-start = ((s32[128,64,1]{1,2,0:T(1,128)}), s32[128,64,1]{1,2,0:T(1,128)}, u32[]{:S(2)}, u32[]{:S(2)}) async-start(s32[128,64,1]{1,2,0:T(1,128)} %bitcast.7), calls=%async_computation | async-start | bytes 131072 | tf_op jit(solution)/shard_map/all_to_all | solution.py:120
  37.5 0.9 fusion.93
  38.4 2.3 collective-permute-start.3
  40.7 3.3 %collective-permute-start.2 = (f32[4,32,3,128]{3,2,1,0:T(4,128)}, f32[4,32,3,128]{3,2,1,0:T(4,128)}, u32[]{:S(2)}, u32[]{:S(2)}) collective-permute-start(f32[4,32,3,128]{3,2,1,0:T(4,128)} %get-tuple-element.28), channel_id=1, source_target_pairs={{0,1},{1,2},{2,3},{3,4},{4,5},{5,6},{6,7},{8,9},{9,10},{10,11},{11... | collective-permute-start | bytes 589832 | tf_op jit(solution)/shard_map/ppermute | solution.py:21
  44.0 0.8 fusion.94
  44.8 1.3 collective-permute-start
  46.1 4.7 %collective-permute-start.1 = (f32[4,3,32,128]{3,2,1,0:T(8,128)}, f32[4,3,32,128]{3,2,1,0:T(8,128)}, u32[]{:S(2)}, u32[]{:S(2)}) collective-permute-start(f32[4,3,32,128]{3,2,1,0:T(8,128)} %get-tuple-element.31), channel_id=1, source_target_pairs={{0,8},{8,16},{16,24},{24,32},{32,40},{40,48},{48,56},{56,64},{64,7... | collective-permute-start | bytes 589832 | tf_op jit(solution)/shard_map/ppermute | solution.py:21
  50.7 0.6 fusion.96
  51.3 1.3 collective-permute-start.4
  52.6 0.9 fusion.92
  53.5 0.5 iota_add_fusion.1
  54.1 0.6 iota_compare_fusion.5
  54.7 0.6 broadcast_clamp_fusion.1
  55.3 0.5 reduce_sum.32
  55.8 0.8 fusion.71
  56.6 0.5 broadcast_multiply_fusion.2
  57.3 1.3 compare_and_fusion.1
  58.6 1.4 convolution_bitcast_fusion
  60.0 1.0 pad_maximum_fusion
  61.0 4.7 %copy.98 = f32[6,128,128]{0,2,1:T(8,128)} copy(f32[6,128,128]{2,1,0:T(8,128)S(1)} %pad_maximum_fusion) | data formatting | bytes 786432 | tf_op jit(solution)/shard_map/concatenate | solution.py:124
  65.9 1.6 copy.94
  67.5 1.0 copy.103
  68.8 0.5 broadcast.276
  69.3 1.6 reduce.7
  71.1 31.1 %gather_fusion = f32[8192,6]{1,0:T(8,128)} fusion(f32[6,16384]{0,1:T(8,128)} %bitcast.50, s32[8192]{0:T(1024)S(1)} %broadcast_clamp_fusion), kind=kCustom, calls=%fused_computation | custom fusion | bytes 425984 | tf_op jit(solution)/shard_map/jit(_take)/gather | solution.py:125
  102.3 3.0 %copy.99 = f32[6,128,64]{2,0,1:T(8,128)S(1)} copy(f32[6,128,64]{0,2,1:T(8,128)} %bitcast.53) | data formatting | bytes 393216 | tf_op jit(solution)/shard_map/jit(_take)/gather | solution.py:125
  105.3 0.9 compare_and_fusion
  106.1 0.9 fusion.97
  107.0 2.0 reshape.210
  109.0 12.1 %all-to-all-start.1 = ((f32[128,1,384]{2,1,0:T(1,128)}), f32[128,1,384]{2,1,0:T(1,128)S(1)}, u32[]{:S(2)}, u32[]{:S(2)}) async-start(f32[128,1,384]{2,1,0:T(1,128)} %reshape.210), calls=%async_computation.1 | async-start | bytes 393216 | tf_op jit(solution)/shard_map/all_to_all | solution.py:126
  121.2 3.9 %collective-permute-start.5 = (f32[3,1,128]{2,1,0:T(1,128)}, f32[3,1,128]{2,1,0:T(1,128)}, u32[]{:S(2)}, u32[]{:S(2)}) collective-permute-start(f32[3,1,128]{2,1,0:T(1,128)} %get-tuple-element.36), channel_id=1, source_target_pairs={{0,8},{8,16},{16,24},{24,32},{32,40},{40,48},{48,56},{56,64},{64,7... | collective-permute-start | bytes 4616 | tf_op jit(solution)/shard_map/ppermute | solution.py:21
  125.1 1.5 select_maximum_fusion
  126.7 0.9 constant_dynamic-update-slice_fusion.3
  127.6 0.6 constant_dynamic-update-slice_fusion.1
  128.3 1.9 fusion.3
  130.1 1.6 fusion.18
  132.3 1.1 reduce.8
  133.5 2.7 %copy.100 = f32[6,128,64]{0,2,1:T(8,128)} copy(f32[6,128,64]{2,0,1:T(8,128)S(1)} %bitcast.57) | data formatting | bytes 393216 | tf_op jit(solution)/shard_map/all_to_all | solution.py:126
  136.3 16.4 %gather_fusion.1 = f32[4096,6]{1,0:T(8,128)} fusion(f32[6,8192]{0,1:T(8,128)} %bitcast.52, s32[4096]{0:T(1024)S(1)} %copy-done.8), kind=kCustom, calls=%fused_computation.1 | custom fusion | bytes 212992 | tf_op jit(solution)/shard_map/jit(_take)/gather | solution.py:127
  152.7 7.5 %multiply_reduce_fusion = f32[6,1024]{0,1:T(8,128)S(1)} fusion(f32[6,1024,4]{0,2,1:T(4,128)} %bitcast.54, f32[1024,4]{1,0:T(8,128)S(1)} %copy.101, pred[1024,4]{1,0:T(8,128)(4,1)S(1)} %copy-done.6), kind=kLoop, calls=%fused_computation.28 | loop fusion | flops 67584 | bytes 143360 | tf_op jit(solution)/shard_map/reduce_sum | solution.py:128
  160.6 1.5 fusion.16
  162.1 2.0 copy.102
  164.2 2.5 fusion.26
  167.2 1.3 copy-done.1
  169.4 14.9 %scatter_custom_fusion.1 = f32[3,8192]{0,1:T(8,128)} fusion(s32[4096]{0:T(1024)} %bitcast.68, f32[3,4096]{0,1:T(8,128)S(1)} %bitcast.51, f32[]{:T(128)} %constant.27.clone.1, f32[4096]{0:T(1024)S(1)} %mul.202), kind=kCustom, calls=%fused_computation.24 | custom fusion | flops 12288 | bytes 164352 | tf_op jit(solution)/shard_map/scatter | solution.py:141
  184.3 3.0 %copy.106 = f32[3,128,64]{2,0,1:T(4,128)S(1)} copy(f32[3,128,64]{0,2,1:T(8,128)} %bitcast.49) | data formatting | bytes 196608 | tf_op jit(solution)/shard_map/all_to_all | solution.py:142
  187.3 0.9 reshape.212
  188.2 9.4 %all-to-all-start.2 = ((f32[128,1,192]{2,1,0:T(1,128)}), f32[128,1,192]{2,1,0:T(1,128)S(1)}, u32[]{:S(2)}, u32[]{:S(2)}) async-start(f32[128,1,192]{2,1,0:T(1,128)} %reshape.212), calls=%async_computation.2 | async-start | bytes 262144 | tf_op jit(solution)/shard_map/all_to_all | solution.py:142
  197.8 3.1 %collective-permute-start.7 = (f32[3,128,1]{2,1,0:T(8,128)S(1)}, f32[3,128,1]{2,1,0:T(8,128)S(1)}, u32[]{:S(2)}, u32[]{:S(2)}) collective-permute-start(f32[3,128,1]{2,1,0:T(8,128)S(1)} %get-tuple-element.35), channel_id=1, source_target_pairs={{0,1},{1,2},{2,3},{3,4},{4,5},{5,6},{6,7},{8,9},{9,10},{10,11},{11... | collective-permute-start | bytes 4616 | tf_op jit(solution)/shard_map/ppermute | solution.py:21
  200.9 2.1 collective-permute-start.6
  203.0 0.8 copy.110
  203.9 1.9 all-to-all-done.2
  205.8 1.0 reduce.9
  207.1 2.6 copy.108
  209.7 54.6 %scatter_custom_fusion.2 = f32[3,16384]{0,1:T(8,128)} fusion(s32[8192]{0:T(1024)} %bitcast.65, f32[8192,3]{1,0:T(8,128)} %copy.108, f32[]{:T(128)} %constant.27.clone.1), kind=kCustom, calls=%fused_computation.5 | custom fusion | flops 24576 | bytes 197120 | tf_op jit(solution)/shard_map/scatter-add | solution.py:146
  264.3 5.3 %copy.109 = f32[3,128,128]{2,1,0:T(8,128)S(1)} copy(f32[3,128,128]{0,2,1:T(8,128)} %bitcast.48) | data formatting | bytes 393216 | tf_op jit(solution)/shard_map/reshape | solution.py:147
  269.6 1.7 multiply_add_fusion
  (74 shorter events, 5.8 us)
Async XLA Ops:
  4.4 2.6 copy-start.10
  7.0 30.6 %copy-start = (f32[4,32,32,128]{3,2,1,0:T(8,128)S(1)}, f32[4,32,32,128]{3,2,1,0:T(8,128)}, u32[]{:S(2)}) copy-start(f32[4,32,32,128]{3,2,1,0:T(8,128)} %param.7) | copy-start | bytes 6291460
  7.5 43.3 %copy-start.2 = (f32[3,128,128]{2,1,0:T(8,128)S(1)}, f32[3,128,128]{2,1,0:T(8,128)}, u32[]{:S(2)}) copy-start(f32[3,128,128]{2,1,0:T(8,128)} %param.8) | copy-start | bytes 589828
  10.2 44.5 %copy-start.9 = (s32[4096,1]{0,1:T(1,128)}, s32[4096,1]{0,1:T(1,128)S(1)}, u32[]{:S(2)}) copy-start(s32[4096,1]{0,1:T(1,128)S(1)} %compare_select_fusion.2) | copy-start | bytes 49156
  26.4 42.3 %all-to-all-start = ((s32[128,64,1]{1,2,0:T(1,128)}), s32[128,64,1]{1,2,0:T(1,128)}, u32[]{:S(2)}, u32[]{:S(2)}) async-start(s32[128,64,1]{1,2,0:T(1,128)} %bitcast.7), calls=%async_computation | async-start | bytes 131072 | tf_op jit(solution)/shard_map/all_to_all | solution.py:120
  38.4 82.7 %collective-permute-start.3 = (f32[4,32,3,128]{3,2,1,0:T(4,128)}, f32[4,32,3,128]{3,2,1,0:T(4,128)}, u32[]{:S(2)}, u32[]{:S(2)}) collective-permute-start(f32[4,32,3,128]{3,2,1,0:T(4,128)} %get-tuple-element.29), channel_id=1, source_target_pairs={{1,0},{2,1},{3,2},{4,3},{5,4},{6,5},{7,6},{9,8},{10,9},{11,10},{12... | collective-permute-start | bytes 589832 | tf_op jit(solution)/shard_map/ppermute | solution.py:22
  40.7 84.3 %collective-permute-start.2 = (f32[4,32,3,128]{3,2,1,0:T(4,128)}, f32[4,32,3,128]{3,2,1,0:T(4,128)}, u32[]{:S(2)}, u32[]{:S(2)}) collective-permute-start(f32[4,32,3,128]{3,2,1,0:T(4,128)} %get-tuple-element.28), channel_id=1, source_target_pairs={{0,1},{1,2},{2,3},{3,4},{4,5},{5,6},{6,7},{8,9},{9,10},{10,11},{11... | collective-permute-start | bytes 589832 | tf_op jit(solution)/shard_map/ppermute | solution.py:21
  44.8 80.3 %collective-permute-start = (f32[4,3,32,128]{3,2,1,0:T(8,128)}, f32[4,3,32,128]{3,2,1,0:T(8,128)S(1)}, u32[]{:S(2)}, u32[]{:S(2)}) collective-permute-start(f32[4,3,32,128]{3,2,1,0:T(8,128)} %get-tuple-element.30), channel_id=1, source_target_pairs={{8,0},{16,8},{24,16},{32,24},{40,32},{48,40},{56,48},{64,56},{72,6... | collective-permute-start | bytes 589832 | tf_op jit(solution)/shard_map/ppermute | solution.py:22
  46.1 79.0 %collective-permute-start.1 = (f32[4,3,32,128]{3,2,1,0:T(8,128)}, f32[4,3,32,128]{3,2,1,0:T(8,128)}, u32[]{:S(2)}, u32[]{:S(2)}) collective-permute-start(f32[4,3,32,128]{3,2,1,0:T(8,128)} %get-tuple-element.31), channel_id=1, source_target_pairs={{0,8},{8,16},{16,24},{24,32},{32,40},{40,48},{48,56},{56,64},{64,7... | collective-permute-start | bytes 589832 | tf_op jit(solution)/shard_map/ppermute | solution.py:21
  51.3 218.2 %collective-permute-start.4 = (f32[3,1,128]{2,1,0:T(1,128)}, f32[3,1,128]{2,1,0:T(1,128)}, u32[]{:S(2)}, u32[]{:S(2)}) collective-permute-start(f32[3,1,128]{2,1,0:T(1,128)} %get-tuple-element.37), channel_id=1, source_target_pairs={{8,0},{16,8},{24,16},{32,24},{40,32},{48,40},{56,48},{64,56},{72,6... | collective-permute-start | bytes 4616 | tf_op jit(solution)/shard_map/ppermute | solution.py:22
  61.0 4.7 %copy-start.11 = (f32[1024,4]{0,1:T(4,128)S(1)}, f32[1024,4]{0,1:T(4,128)}, u32[]{:S(2)}) copy-start(f32[1024,4]{0,1:T(4,128)} %param.12) | copy-start | bytes 49156
  71.1 31.2 %copy-start.7 = (s32[8192,1]{0,1:T(1,128)}, s32[8192,1]{0,1:T(1,128)S(1)}, u32[]{:S(2)}) copy-start(s32[8192,1]{0,1:T(1,128)S(1)} %compare_select_fusion) | copy-start | bytes 98308
  109.0 22.8 %all-to-all-start.1 = ((f32[128,1,384]{2,1,0:T(1,128)}), f32[128,1,384]{2,1,0:T(1,128)S(1)}, u32[]{:S(2)}, u32[]{:S(2)}) async-start(f32[128,1,384]{2,1,0:T(1,128)} %reshape.210), calls=%async_computation.1 | async-start | bytes 393216 | tf_op jit(solution)/shard_map/all_to_all | solution.py:126
  121.2 148.4 %collective-permute-start.5 = (f32[3,1,128]{2,1,0:T(1,128)}, f32[3,1,128]{2,1,0:T(1,128)}, u32[]{:S(2)}, u32[]{:S(2)}) collective-permute-start(f32[3,1,128]{2,1,0:T(1,128)} %get-tuple-element.36), channel_id=1, source_target_pairs={{0,8},{8,16},{16,24},{24,32},{32,40},{40,48},{48,56},{56,64},{64,7... | collective-permute-start | bytes 4616 | tf_op jit(solution)/shard_map/ppermute | solution.py:21
  133.5 2.8 %copy-start.8 = (s32[4096]{0:T(1024)S(1)}, s32[4096]{0:T(1024)}, u32[]{:S(2)}) copy-start(s32[4096]{0:T(1024)} %broadcast_clamp_fusion.1) | copy-start | bytes 49156
  133.5 19.2 %copy-start.6 = (pred[1024,4]{1,0:T(8,128)(4,1)S(1)}, pred[1024,4]{1,0:T(8,128)(4,1)}, u32[]{:S(2)}) copy-start(pred[1024,4]{1,0:T(8,128)(4,1)} %copy.94) | copy-start | bytes 12292
  152.7 7.9 %copy-start.4 = (f32[1,32,32,128]{3,2,1,0:T(8,128)S(1)}, f32[1,32,32,128]{3,2,1,0:T(8,128)}, u32[]{:S(2)}) copy-start(f32[1,32,32,128]{3,2,1,0:T(8,128)} %get-tuple-element.26) | copy-start | bytes 1572868
  152.7 8.0 %copy-start.13 = (s32[128]{0:T(128)S(1)}, s32[128]{0:T(128)}, u32[]{:S(2)}) copy-start(s32[128]{0:T(128)} %iota_add_fusion.1) | copy-start | bytes 1540
  152.7 8.0 %copy-start.14 = (pred[128]{0:T(512)(128)(4,1)S(1)}, pred[128]{0:T(512)(128)(4,1)}, u32[]{:S(2)}) copy-start(pred[128]{0:T(512)(128)(4,1)} %iota_compare_fusion.5) | copy-start | bytes 388
  152.7 8.0 %copy-start.15 = (f32[128]{0:T(128)S(1)}, f32[128]{0:T(128)}, u32[]{:S(2)}) copy-start(f32[128]{0:T(128)} %broadcast_multiply_fusion.2) | copy-start | bytes 1540
  160.2 3.9 %copy-start.3 = (f32[1024,128]{1,0:T(8,128)S(1)}, f32[1024,128]{1,0:T(8,128)}, u32[]{:S(2)}) copy-start(f32[1024,128]{1,0:T(8,128)} %copy.103) | copy-start | bytes 1572868
  166.7 2.1 copy-start.12
  167.2 1.3 copy-start.1
  188.2 17.6 %all-to-all-start.2 = ((f32[128,1,192]{2,1,0:T(1,128)}), f32[128,1,192]{2,1,0:T(1,128)S(1)}, u32[]{:S(2)}, u32[]{:S(2)}) async-start(f32[128,1,192]{2,1,0:T(1,128)} %reshape.212), calls=%async_computation.2 | async-start | bytes 262144 | tf_op jit(solution)/shard_map/all_to_all | solution.py:142
  197.8 71.8 %collective-permute-start.7 = (f32[3,128,1]{2,1,0:T(8,128)S(1)}, f32[3,128,1]{2,1,0:T(8,128)S(1)}, u32[]{:S(2)}, u32[]{:S(2)}) collective-permute-start(f32[3,128,1]{2,1,0:T(8,128)S(1)} %get-tuple-element.35), channel_id=1, source_target_pairs={{0,1},{1,2},{2,3},{3,4},{4,5},{5,6},{6,7},{8,9},{9,10},{10,11},{11... | collective-permute-start | bytes 4616 | tf_op jit(solution)/shard_map/ppermute | solution.py:21
  200.9 68.7 %collective-permute-start.6 = (f32[3,128,1]{2,1,0:T(8,128)S(1)}, f32[3,128,1]{2,1,0:T(8,128)S(1)}, u32[]{:S(2)}, u32[]{:S(2)}) collective-permute-start(f32[3,128,1]{2,1,0:T(8,128)S(1)} %get-tuple-element.34), channel_id=1, source_target_pairs={{1,0},{2,1},{3,2},{4,3},{5,4},{6,5},{7,6},{9,8},{10,9},{11,10},{12... | collective-permute-start | bytes 4616 | tf_op jit(solution)/shard_map/ppermute | solution.py:22
  264.3 5.3 %copy-start.5 = (f32[3,128,128]{2,1,0:T(8,128)S(1)}, f32[3,128,128]{2,1,0:T(8,128)}, u32[]{:S(2)}) copy-start(f32[3,128,128]{2,1,0:T(8,128)} %param.9) | copy-start | bytes 589828
where the time goes:
time: 274 us; the launch traced here: 271 us
  local copies, waits for them, and re-layouts  109 us (40%)
  other arithmetic  102 us (37%)
  starting transfers between devices  54.6 us (20%)
  matrix products  2.87 us (1%)
    scatter-add x1, other arithmetic, body(): shell_force = jnp.zeros((3, rows_x * rows_y), jnp.float32).at[:, asked_no...  54.6 us
    gather x2, local copies, waits for them, and re-layouts, body(): picked = jnp.take(stacked, asked_nodes, axis=1)  34.1 us
    gather x1, local copies, waits for them, and re-layouts, body(): motion = jnp.take(replies, slot_index, axis=1).reshape(6, points, stencil)  16.4 us
    scatter x1, local copies, waits for them, and re-layouts, body(): jnp.zeros((devices * capacity,), jnp.int32).at[slot_index].set(node_ids)  15.5 us
    ppermute x4, starting transfers between devices, with_halo(): lax.ppermute(last, axis, up)  14.9 us
    scatter x1, other arithmetic, body(): jnp.zeros((3, devices * capacity), jnp.float32).at[:, slot_index]  14.9 us
    all_to_all x1, starting transfers between devices, body(): lax.all_to_all(picked, ('span', 'chord'), split_axis=1, concat_axis=1, ti...  12.1 us
    all_to_all x1, starting transfers between devices, body(): lax.all_to_all(requests, ('span', 'chord'), split_axis=0, concat_axis=0,...  11.1 us
  transfers between devices with their start and end apart: 11, of which 1 were waited for; matrix products, arithmetic and copies ran while one was open for 68% of the time, Pallas kernels for 0%

commit v1 on v0

v1 whole, which is shorter than its diff:
```python
import jax
import jax.numpy as jnp
from jax import lax
from jax.experimental import pallas as pl
from jax.experimental.pallas import tpu as pltpu
from jax.sharding import PartitionSpec as P

MESH = pl.DeviceIdType.MESH
F32, BF16, I32 = jnp.float32, jnp.bfloat16, jnp.int32
NS, NC, ND = 16, 8, 128
CAP = 64
CX, CY, NZ = 32, 32, 128
PTS, K = 1024, 4
ENT = PTS * K
SLOTS = ND * CAP
QW = 256
SCALE = 0.4 / 60.0
NT = (((1,), (1,)), ((), ()))


def iota(shape, dim):
    return lax.broadcasted_iota(I32, shape, dim)


def split(value):
    high = value.astype(BF16)
    return high, (value - high.astype(F32)).astype(BF16)


def dot(a, b):
    return jnp.dot(a, b, preferred_element_type=F32)


def dot_nt(a, b):
    return lax.dot_general(a, b, NT, preferred_element_type=F32)


def diff(far_up, mid_up, up, down, mid_down, far_down):
    return 45.0 * (up - down) - 9.0 * (mid_up - mid_down) + (far_up - far_down)


def stencil(distance):
    size = jnp.abs(distance)
    value = jnp.where(size == 1, 45.0, jnp.where(size == 2, -9.0, jnp.where(size == 3, 1.0, 0.0)))
    return jnp.where(distance > 0, value, -value)


def kernel(
    own_ref, node_ref, w_ref, nrm_ref, fluid_hbm, disp_hbm, vel_hbm,
    fluid_out, motion_ref, disp_out, vel_out,
    xbuf, ybuf, fo, zb, dbuf, vbuf,
    onehot, rank, reqb, req, asked, px, py,
    table, ohy, ohx, picked, rep, got, lookup, p0,
    loadb, outg, arrived, vals, fb, force, colsend, collow, colhigh,
    in_sem, out_sem, halo_s, halo_r, a2a_s, a2a_r,
):
    span, chord = lax.axis_index("span"), lax.axis_index("chord")
    me = span * NC + chord

    def place(p):
        return (p // NC, lax.rem(p, NC))

    loads = [
        pltpu.make_async_copy(disp_hbm, dbuf.at[:, pl.ds(8, 128)], in_sem.at[0]),
        pltpu.make_async_copy(vel_hbm, vbuf, in_sem.at[1]),
        pltpu.make_async_copy(fluid_hbm, xbuf.at[:, pl.ds(3, CX)], in_sem.at[2]),
        pltpu.make_async_copy(fluid_hbm.at[0], ybuf.at[0, :, pl.ds(8, CY)], in_sem.at[3]),
        pltpu.make_async_copy(fluid_hbm.at[2], ybuf.at[1, :, pl.ds(8, CY)], in_sem.at[4]),
    ]
    for c in loads:
        c.start()

    barrier = pltpu.get_barrier_semaphore()

    def greet(d, carry):
        pl.semaphore_signal(barrier, 1, device_id=place(lax.rem(me + d, ND)), device_id_type=MESH)
        return carry

    lax.fori_loop(1, ND, greet, 0)

    before = (iota((QW, QW), 0) < iota((QW, QW), 1)).astype(F32).astype(BF16)
    ones = jnp.ones((QW, QW), BF16)
    sub_o = iota((ND, QW), 0)
    sub_s = iota((CAP, QW), 0)
    offset = jnp.zeros((ND, QW), F32)
    for q in range(PTS // QW):
        cols = slice(q * QW, (q + 1) * QW)
        masks = []
        count = jnp.zeros((ND, QW), F32)
        for k in range(K):
            mask = sub_o == own_ref[k : k + 1, cols]
            masks.append(mask)
            hot = jnp.where(mask, 1.0, 0.0)
            onehot[:, k * PTS + q * QW : k * PTS + (q + 1) * QW] = hot.astype(BF16)
            count = count + hot
        count = count.astype(BF16)
        prior = dot(count, before) + offset
        offset = offset + dot(count, ones)
        for k in range(K):
            slot = jnp.sum(jnp.where(masks[k], prior, 0.0), axis=0, keepdims=True).astype(I32)
            rank[k : k + 1, cols] = slot
            node = node_ref[k : k + 1, cols]
            at = sub_s == slot
            ent = slice(k * PTS + q * QW, k * PTS + (q + 1) * QW)
            reqb[0:CAP, ent] = jnp.where(at, (node // 128).astype(F32), 0.0).astype(BF16)
            reqb[CAP:, ent] = jnp.where(at, lax.rem(node, 128).astype(F32), 0.0).astype(BF16)
    req[0] = dot_nt(onehot[...], reqb[...])

    pl.semaphore_wait(barrier, ND - 1)

    def exchange(src, dst, index):
        def send(d, carry):
            p = lax.rem(me + d, ND)
            pltpu.make_async_remote_copy(
                src.at[:, pl.ds(p, 1)], dst.at[:, pl.ds(me, 1)], a2a_s.at[index], a2a_r.at[index],
                device_id=place(p), device_id_type=MESH,
            ).start()
            return carry

        lax.fori_loop(1, ND, send, 0)
        dst[:, pl.ds(me, 1), :] = src[:, pl.ds(me, 1), :]

    def whole(src, dst, index):
        return pltpu.make_async_remote_copy(
            src.at[:, pl.ds(0, ND - 1)], dst.at[:, pl.ds(0, ND - 1)], a2a_s.at[index], a2a_r.at[index],
            device_id=place(me), device_id_type=MESH,
        )

    exchange(req, asked, 0)

    for c in loads:
        c.wait()
    for c in range(3):
        turned = dbuf[c, 8:136, :].T
        colsend[0, c : c + 1, :] = turned[0:1, :]
        colsend[1, c : c + 1, :] = turned[127:128, :]
    up = (lax.rem(span + 1, NS), chord)
    down = (lax.rem(span + NS - 1, NS), chord)
    right = (span, lax.rem(chord + 1, NC))
    left = (span, lax.rem(chord + NC - 1, NC))
    moves = [
        (xbuf.at[:, pl.ds(CX, 3)], xbuf.at[:, pl.ds(0, 3)], up),
        (xbuf.at[:, pl.ds(3, 3)], xbuf.at[:, pl.ds(CX + 3, 3)], down),
        (ybuf.at[:, :, pl.ds(CY + 5, 3)], ybuf.at[:, :, pl.ds(5, 3)], right),
        (ybuf.at[:, :, pl.ds(8, 3)], ybuf.at[:, :, pl.ds(CY + 8, 3)], left),
        (dbuf.at[:, pl.ds(135, 1)], dbuf.at[:, pl.ds(7, 1)], up),
        (dbuf.at[:, pl.ds(8, 1)], dbuf.at[:, pl.ds(136, 1)], down),
        (colsend.at[1], collow, right),
        (colsend.at[0], colhigh, left),
    ]
    halos = [
        pltpu.make_async_remote_copy(a, b, halo_s.at[i], halo_r.at[i], device_id=to, device_id_type=MESH)
        for i, (a, b, to) in enumerate(moves)
    ]
    for h in halos:
        h.start()

    for c in range(6):
        value = dbuf[c, 8:136, :] if c < 3 else vbuf[c - 3]
        high, low = split(value)
        table[c * 128 : (c + 1) * 128, 0:128] = high
        table[c * 128 : (c + 1) * 128, 128:256] = low

    src, tgt = iota((NZ, NZ), 0), iota((NZ, NZ), 1)
    inner = stencil(src - tgt)
    ghost = jnp.where(src < 3, stencil(-(src + 1 + tgt)), 0.0)
    for i, (f, tab) in enumerate(((0, inner + ghost), (3, inner - ghost))):
        tab = tab.astype(BF16)
        tab = jnp.concatenate([tab, tab], axis=0)
        for b in range(4):
            high, low = split(xbuf[f, 3 + 8 * b : 11 + 8 * b].reshape(256, NZ))
            zb[i, b * 256 : (b + 1) * 256, :] = dot(jnp.concatenate([high, low], axis=1), tab)

    first = whole(req, asked, 0)
    first.wait_recv()
    lane = iota((CAP, 128), 1)
    a, b = asked[0, 0:64, :], asked[0, 64:128, :]
    ar, br = pltpu.roll(a, 64, 1), pltpu.roll(b, 64, 1)
    px[...] = jnp.where(lane < 64, a, br).astype(I32)
    py[...] = jnp.where(lane < 64, ar, b).astype(I32)

    lane8 = iota((8, 128), 1)

    def pick(g0, carry):
        g = lax.rem(g0 + span, 8)
        rows = pl.ds(pl.multiple_of(g * 8, 8), 8)
        xs, ys = px[rows, :], py[rows, :]
        for t in range(4):
            yrow = jnp.concatenate([ys[2 * t : 2 * t + 1], ys[2 * t + 1 : 2 * t + 2]], axis=1)
            xrow = jnp.concatenate([xs[2 * t : 2 * t + 1], xs[2 * t + 1 : 2 * t + 2]], axis=1)
            hot = jnp.where(sub_o == yrow, 1.0, 0.0).astype(BF16)
            ohy[:, pl.ds(pl.multiple_of((g * 4 + t) * QW, QW), QW)] = hot
            out = dot(table[...], jnp.concatenate([hot, hot], axis=0))
            mask = sub_o == xrow
            for c in range(6):
                row = jnp.sum(jnp.where(mask, out[c * 128 : (c + 1) * 128], 0.0), axis=0, keepdims=True)
                picked[c, 2 * t : 2 * t + 1, :] = row[:, 0:128]
                picked[c, 2 * t + 1 : 2 * t + 2, :] = row[:, 128:256]
        high_rows = pl.ds(pl.multiple_of(g * 8 + 64, 8), 8)
        for j in range(3):
            even, odd = picked[2 * j], picked[2 * j + 1]
            rep[j, rows, :] = jnp.where(lane8 < 64, even, pltpu.roll(odd, 64, 1))
            rep[j, high_rows, :] = jnp.where(lane8 < 64, pltpu.roll(even, 64, 1), odd)

        def reply(i, inner_carry):
            p = g * 8 + lax.rem(i, 8) + (i // 8) * 64

            @pl.when(p != me)
            def _():
                pltpu.make_async_remote_copy(
                    rep.at[:, pl.ds(p, 1)], got.at[:, pl.ds(me, 1)], a2a_s.at[1], a2a_r.at[1],
                    device_id=place(p), device_id_type=MESH,
                ).start()

            return inner_carry

        lax.fori_loop(0, 16, reply, 0)
        return carry

    lax.fori_loop(0, 8, pick, 0)
    got[:, pl.ds(me, 1), :] = rep[:, pl.ds(me, 1), :]

    for h in halos:
        h.wait_recv()

    @pl.when(span == 0)
    def _():
        xbuf[:, 0:3] = jnp.zeros((4, 3, CY, NZ), F32)
        dbuf[:, 7:8, :] = jnp.zeros((3, 1, 128), F32)

    @pl.when(span == NS - 1)
    def _():
        xbuf[:, CX + 3 : CX + 6] = jnp.zeros((4, 3, CY, NZ), F32)
        dbuf[:, 136:137, :] = jnp.zeros((3, 1, 128), F32)

    @pl.when(chord == 0)
    def _():
        ybuf[:, :, 5:8, :] = jnp.zeros((2, CX, 3, NZ), F32)
        collow[...] = jnp.zeros((8, 128), F32)

    @pl.when(chord == NC - 1)
    def _():
        ybuf[:, :, CY + 8 : CY + 11, :] = jnp.zeros((2, CX, 3, NZ), F32)
        colhigh[...] = jnp.zeros((8, 128), F32)

    def plane(x, carry):
        def dx(f):
            return diff(*[xbuf[f, x + 3 + o] for o in (3, 2, 1, -1, -2, -3)])

        def dy(f):
            return diff(*[ybuf[f, x, 8 + o : 8 + CY + o, :] for o in (3, 2, 1, -1, -2, -3)])

        zrows = pl.ds(pl.multiple_of(x * CY, CY), CY)
        dp, du = dx(0), dx(1)
        fo[0, x] = xbuf[0, x + 3] - SCALE * (0.5 * dp + du + dy(1) + zb[1, zrows, :])
        fo[1, x] = xbuf[1, x + 3] - SCALE * (0.5 * du + dp)
        fo[2, x] = xbuf[2, x + 3] - SCALE * (0.5 * dx(2) + dy(0))
        fo[3, x] = xbuf[3, x + 3] - SCALE * (0.5 * dx(3) + zb[0, zrows, :])
        return carry

    lax.fori_loop(0, CX, plane, 0)
    flow_out = pltpu.make_async_copy(fo.at[pl.ds(1, 3)], fluid_out.at[pl.ds(1, 3)], out_sem.at[0])
    flow_out.start()
    for b in range(8):
        turned = fo[0, 4 * b : 4 * b + 4].reshape(128, NZ).T
        p0[0:1, b * 128 : (b + 1) * 128] = turned[0:1, :]

    def columns(g, carry):
        rows = pl.ds(pl.multiple_of(g * 8, 8), 8)
        xs = px[rows, :]
        for t in range(8):
            hot = jnp.where(sub_o[:, 0:128] == xs[t : t + 1], 1.0, 0.0).astype(BF16)
            ohx[:, pl.ds(pl.multiple_of((g * 8 + t) * 128, 128), 128)] = hot
        return carry

    lax.fori_loop(0, 8, columns, 0)

    second = whole(rep, got, 1)
    second.wait_recv()
    for j in range(3):
        high, low = split(got[j].T)
        lookup[j * 128 : (j + 1) * 128, 0:128] = high
        lookup[j * 128 : (j + 1) * 128, 128:256] = low

    def interp(q, carry):
        cols = pl.ds(pl.multiple_of(q * QW, QW), QW)
        totals = [jnp.zeros((8, QW), F32) for _ in range(6)]
        for k in range(K):
            hot = onehot[:, pl.ds(pl.multiple_of(k * PTS + q * QW, QW), QW)]
            out = dot(lookup[...], jnp.concatenate([hot, hot], axis=0))
            at = sub_s == rank[k : k + 1, cols]
            weight = w_ref[k : k + 1, cols]
            for c in range(6):
                part = jnp.where(at, out[c * CAP : (c + 1) * CAP], 0.0)
                totals[c] = totals[c] + weight * jnp.sum(part.reshape(8, 8, QW), axis=0)
        for c in range(6):
            motion_ref[c : c + 1, cols] = jnp.sum(totals[c], axis=0, keepdims=True)
        return carry

    lax.fori_loop(0, PTS // QW, interp, 0)

    pressure = p0[0:1, :] + (SCALE * 74.0) * motion_ref[5:6, :]
    for q in range(PTS // QW):
        cols = slice(q * QW, (q + 1) * QW)
        for k in range(K):
            ent = slice(k * PTS + q * QW, k * PTS + (q + 1) * QW)
            at = sub_s == rank[k : k + 1, cols]
            for c in range(3):
                value = nrm_ref[c : c + 1, cols] * pressure[:, cols] * w_ref[k : k + 1, cols]
                high = value.astype(BF16).astype(F32)
                loadb[c * CAP : (c + 1) * CAP, ent] = jnp.where(at, high, 0.0).astype(BF16)
                loadb[256 + c * CAP : 256 + (c + 1) * CAP, ent] = jnp.where(at, value - high, 0.0).astype(BF16)
    loadb[192:256, :] = jnp.zeros((64, ENT), BF16)
    loadb[448:512, :] = jnp.zeros((64, ENT), BF16)
    both = dot_nt(onehot[...], loadb[...])
    outg[0] = both[:, 0:128] + both[:, 256:384]
    outg[1] = both[:, 128:256] + both[:, 384:512]
    exchange(outg, arrived, 2)

    zlane = iota((128, NZ), 1)
    reach = jnp.where(zlane == 0, 74.0 * SCALE, jnp.where(zlane == 1, -16.0 * SCALE, jnp.where(zlane == 2, 2.0 * SCALE, 0.0)))
    for b in range(8):
        turned = jnp.broadcast_to(motion_ref[5:6, b * 128 : (b + 1) * 128], (8, 128)).T
        fix = (turned[:, 0:1] * reach).reshape(4, CY, NZ)
        fo[0, 4 * b : 4 * b + 4] = fo[0, 4 * b : 4 * b + 4] + fix
    pressure_out = pltpu.make_async_copy(fo.at[0], fluid_out.at[0], out_sem.at[1])
    pressure_out.start()

    third = whole(outg, arrived, 2)
    third.wait_recv()
    for c, j in ((0, 0), (1, 0), (2, 1)):
        a, b = arrived[j, 0:64, :], arrived[j, 64:128, :]
        if c == 1:
            value = jnp.where(lane < 64, pltpu.roll(a, 64, 1), b)
        else:
            value = jnp.where(lane < 64, a, pltpu.roll(b, 64, 1))
        high = value.astype(BF16).astype(F32)
        vals[c] = high
        vals[3 + c] = value - high
    force[...] = jnp.zeros((384, 128), F32)

    def collect(g, carry):
        rows = pl.ds(pl.multiple_of(g * 8, 8), 8)
        cols = pl.ds(pl.multiple_of(g * 1024, 1024), 1024)
        for half in range(2):
            for c in range(3):
                value = vals[half * 3 + c, rows, :]
                for t in range(8):
                    spread = jnp.broadcast_to(value[t : t + 1], (16, 128)).astype(BF16)
                    spread = jnp.concatenate([spread] * 8, axis=0)
                    hot = ohx[:, pl.ds(pl.multiple_of((g * 8 + t) * 128, 128), 128)]
                    fb[c * 128 : (c + 1) * 128, half * 1024 + t * 128 : half * 1024 + (t + 1) * 128] = hot * spread
        hoty = ohy[:, cols]
        force[...] += dot_nt(fb[...], jnp.concatenate([hoty, hoty], axis=1))
        return carry

    lax.fori_loop(0, 8, collect, 0)

    lane128 = iota((128, 128), 1)
    low_t, high_t = collow[...].T, colhigh[...].T
    for c in range(3):
        mid = dbuf[c, 8:136, :]
        west = jnp.where(lane128 == 0, low_t[:, c : c + 1], pltpu.roll(mid, 1, 1))
        east = jnp.where(lane128 == 127, high_t[:, c : c + 1], pltpu.roll(mid, 127, 1))
        lap = dbuf[c, 9:137, :] + dbuf[c, 7:135, :] + east + west - 4.0 * mid
        vel = vbuf[c]
        vel_new = vel + 0.3 * (0.5 * lap + force[c * 128 : (c + 1) * 128, :] - 0.2 * vel)
        vel_out[c] = vel_new
        disp_out[c] = mid + 0.3 * vel_new

    for h in halos:
        h.wait_send()
    first.wait_send()
    second.wait_send()
    third.wait_send()
    flow_out.wait()
    pressure_out.wait()


def body(fluid, disp, vel, owners, nodes, weights, normals):
    small = pl.BlockSpec(memory_space=pltpu.VMEM)
    big = pl.BlockSpec(memory_space=pl.ANY)
    vm = pltpu.VMEM
    dma = pltpu.SemaphoreType.DMA
    scratch = [
        vm((4, CX + 6, CY, NZ), F32),
        vm((2, CX, CY + 16, NZ), F32),
        vm((4, CX, CY, NZ), F32),
        vm((2, PTS, NZ), F32),
        vm((3, 144, 128), F32),
        vm((3, 128, 128), F32),
        vm((ND, ENT), BF16),
        vm((K, PTS), I32),
        vm((128, ENT), BF16),
        vm((1, ND, 128), F32),
        vm((1, ND, 128), F32),
        vm((CAP, 128), I32),
        vm((CAP, 128), I32),
        vm((768, 256), BF16),
        vm((128, SLOTS), BF16),
        vm((128, SLOTS), BF16),
        vm((6, 8, 128), F32),
        vm((3, ND, 128), F32),
        vm((3, ND, 128), F32),
        vm((384, 256), BF16),
        vm((8, PTS), F32),
        vm((512, ENT), BF16),
        vm((2, ND, 128), F32),
        vm((2, ND, 128), F32),
        vm((6, CAP, 128), F32),
        vm((384, 2048), BF16),
        vm((384, 128), F32),
        vm((2, 8, 128), F32),
        vm((8, 128), F32),
        vm((8, 128), F32),
        dma((5,)),
        dma((2,)),
        dma((8,)),
        dma((8,)),
        dma((3,)),
        dma((3,)),
    ]
    return pl.pallas_call(
        kernel,
        name="coupling",
        out_shape=(
            jax.ShapeDtypeStruct(fluid.shape, F32),
            jax.ShapeDtypeStruct((6, PTS), F32),
            jax.ShapeDtypeStruct(disp.shape, F32),
            jax.ShapeDtypeStruct(vel.shape, F32),
        ),
        in_specs=[small] * 4 + [big] * 3,
        out_specs=(big, small, small, small),
        scratch_shapes=scratch,
        compiler_params=pltpu.CompilerParams(
            collective_id=0, has_side_effects=True, vmem_limit_bytes=56 * 1024 * 1024
        ),
    )(owners.T, nodes.T, weights.T, normals, fluid, disp, vel)


def solution(mesh):
    block, line = P(None, "span", "chord"), P(("span", "chord"), None)
    return jax.shard_map(
        body,
        mesh=mesh,
        in_specs=(P(None, "span", "chord", None), block, block, line, line, line, P(None, ("span", "chord"))),
        out_specs=(P(None, "span", "chord", None), P(None, ("span", "chord")), block, block),
        check_vma=False,
    )
```

time: 274 us -> 55.7 us (0.20)
  the two profiles are of different devices: /device:TPU:17 before, /device:TPU:1 now
where the time goes in v1:
time: 55.7 us; the launch traced here: 55.5 us
  Pallas kernels  49.7 us (89%)
  local copies, waits for them, and re-layouts  5.11 us (9%)
  between operations  0.67 us (1%)
    pallas_call x1, Pallas kernels, body(): pl.pallas_call(kernel, name='coupling', out_shape=(jax.ShapeDtypeStruct(f...  49.7 us
    unnamed x10, local copies, waits for them, and re-layouts  5.11 us

profile of v1, /device:TPU:1, one launch (start us, length us, event | category | flops | bytes accessed | tf_op | source)
XLA Modules:
  0.0 55.5 jit_solution(17825301732784768304)
XLA Ops:
  0.6 49.7 %coupling.1 = (f32[4,32,32,128]{3,2,1,0:T(8,128)}, f32[6,1024]{1,0:T(8,128)}, f32[3,128,128]{2,1,0:T(8,128)}, f32[3,128,128]{2,1,0:T(8,128)}) custom-call(s32[4,1024]{1,0:T(4,128)} %bitcast.3, s32[4,1024]{1,0:T(4,128)} %bitcast.4, f32[4,1024]{1,0:T(4,128)} %bitcast.5, f32[3,1024]{1,0:T(4,128)} %nrm_ref.1, f32[4,32,32,128]{3,2,1,0:T(8,128)} %fluid_hbm.1, ...), custom_call_target="tpu_custom_call" | custom-call | tf_op jit(solution)/shard_map/coupling/pallas_call | solution.py:423
  50.4 0.0 copy-start.2
  50.4 0.0 copy-start.1
  50.4 0.0 copy-start
  50.4 3.1 %copy.15 = f32[4,32,32,128]{3,2,1,0:T(8,128)} copy(f32[4,32,32,128]{3,2,1,0:T(8,128)} %get-tuple-element.8) | data formatting | bytes 4194304
  53.5 0.0 copy-done.2
  53.5 0.6 %copy.16 = f32[6,1024]{1,0:T(8,128)} copy(f32[6,1024]{1,0:T(8,128)S(1)} %copy-done.2) | data formatting | bytes 49152
  54.1 0.0 copy-done.1
  54.1 0.7 %copy.17 = f32[3,128,128]{2,1,0:T(8,128)} copy(f32[3,128,128]{2,1,0:T(8,128)S(1)} %copy-done.1) | data formatting | bytes 393216
  54.8 0.0 copy-done
  54.8 0.7 %copy.18 = f32[3,128,128]{2,1,0:T(8,128)} copy(f32[3,128,128]{2,1,0:T(8,128)S(1)} %copy-done) | data formatting | bytes 393216
Async XLA Ops:
  50.4 3.2 %copy-start.2 = (f32[6,1024]{1,0:T(8,128)S(1)}, f32[6,1024]{1,0:T(8,128)}, u32[]{:S(2)}) copy-start(f32[6,1024]{1,0:T(8,128)} %get-tuple-element.9) | copy-start | bytes 73732
  50.4 3.8 %copy-start.1 = (f32[3,128,128]{2,1,0:T(8,128)S(1)}, f32[3,128,128]{2,1,0:T(8,128)}, u32[]{:S(2)}) copy-start(f32[3,128,128]{2,1,0:T(8,128)} %get-tuple-element.10) | copy-start | bytes 589828
  50.4 4.4 %copy-start = (f32[3,128,128]{2,1,0:T(8,128)S(1)}, f32[3,128,128]{2,1,0:T(8,128)}, u32[]{:S(2)}) copy-start(f32[3,128,128]{2,1,0:T(8,128)} %get-tuple-element.11) | copy-start | bytes 589828

commit v2 on v1

v2 whole, which is shorter than its diff:
```python
import jax
import jax.numpy as jnp
from jax import lax
from jax.experimental import pallas as pl
from jax.experimental.pallas import tpu as pltpu
from jax.sharding import PartitionSpec as P

MESH = pl.DeviceIdType.MESH
F32, BF16, I32 = jnp.float32, jnp.bfloat16, jnp.int32
NS, NC, ND = 16, 8, 128
CAP = 64
CX, CY, NZ = 32, 32, 128
PTS, K = 1024, 4
ENT = PTS * K
SLOTS = ND * CAP
QW = 256
SCALE = 0.4 / 60.0
NT = (((1,), (1,)), ((), ()))


def iota(shape, dim):
    return lax.broadcasted_iota(I32, shape, dim)


def split(value):
    high = value.astype(BF16)
    return high, (value - high.astype(F32)).astype(BF16)


def dot(a, b):
    return jnp.dot(a, b, preferred_element_type=F32)


def dot_nt(a, b):
    return lax.dot_general(a, b, NT, preferred_element_type=F32)


def diff(far_up, mid_up, up, down, mid_down, far_down):
    return 45.0 * (up - down) - 9.0 * (mid_up - mid_down) + (far_up - far_down)


def stencil(distance):
    size = jnp.abs(distance)
    value = jnp.where(size == 1, 45.0, jnp.where(size == 2, -9.0, jnp.where(size == 3, 1.0, 0.0)))
    return jnp.where(distance > 0, value, -value)


def kernel(
    own_ref, node_ref, w_ref, nrm_ref, fluid_hbm, disp_hbm, vel_hbm,
    fo, motion_ref, disp_out, vel_out,
    xbuf, ybuf, zb, dbuf, vbuf,
    onehot, rank, reqb, req, asked, px,
    table, ohy, ohx, picked, rep, got, lookup, p0,
    loadb, outg, arrived, fb, force, spread, colsend, collow, colhigh,
    in_sem, halo_s, halo_r, sent, ask_r, reply_r, load_r,
):
    span, chord = lax.axis_index("span"), lax.axis_index("chord")
    me = span * NC + chord

    mine = span // 2
    slot_row = mine * 8 + chord + 64 * lax.rem(span, 2)

    loads = [
        pltpu.make_async_copy(disp_hbm, dbuf.at[:, pl.ds(8, 128)], in_sem.at[0]),
        pltpu.make_async_copy(vel_hbm, vbuf, in_sem.at[1]),
        pltpu.make_async_copy(fluid_hbm, xbuf.at[:, pl.ds(3, CX)], in_sem.at[2]),
        pltpu.make_async_copy(fluid_hbm.at[0], ybuf.at[0, :, pl.ds(8, CY)], in_sem.at[3]),
        pltpu.make_async_copy(fluid_hbm.at[2], ybuf.at[1, :, pl.ds(8, CY)], in_sem.at[4]),
    ]
    for c in loads:
        c.start()

    barrier = pltpu.get_barrier_semaphore()

    def far_first(k):
        half = (k + 1) // 2
        return lax.rem(span + 10 + jnp.where(lax.rem(k, 2) == 1, half, 16 - half), NS)

    def each_peer(act):
        def one(k, carry):
            s = far_first(k)

            @pl.when(s != span)
            def _():
                for c in range(NC):
                    act(s, c)

            return carry

        lax.fori_loop(0, NS, one, 0)
        for c in range(NC):

            @pl.when(c != chord)
            def _():
                act(span, c)

    each_peer(lambda s, c: pl.semaphore_signal(barrier, 1, device_id=(s, c), device_id_type=MESH))

    before = (iota((QW, QW), 0) < iota((QW, QW), 1)).astype(F32).astype(BF16)
    ones = jnp.ones((QW, QW), BF16)
    sub_o = iota((ND, QW), 0)
    sub_s = iota((CAP, QW), 0)
    offset = jnp.zeros((ND, QW), F32)
    for q in range(PTS // QW):
        cols = slice(q * QW, (q + 1) * QW)
        masks = []
        count = jnp.zeros((ND, QW), F32)
        for k in range(K):
            mask = sub_o == own_ref[k : k + 1, cols]
            masks.append(mask)
            hot = jnp.where(mask, 1.0, 0.0)
            onehot[:, k * PTS + q * QW : k * PTS + (q + 1) * QW] = hot.astype(BF16)
            count = count + hot
        count = count.astype(BF16)
        prior = dot(count, before) + offset
        offset = offset + dot(count, ones)
        for k in range(K):
            slot = jnp.sum(jnp.where(masks[k], prior, 0.0), axis=0, keepdims=True).astype(I32)
            rank[k : k + 1, cols] = slot
            node = node_ref[k : k + 1, cols]
            at = sub_s == slot
            ent = slice(k * PTS + q * QW, k * PTS + (q + 1) * QW)
            reqb[0:CAP, ent] = jnp.where(at, (node // 256).astype(F32), 0.0).astype(BF16)
            reqb[CAP:, ent] = jnp.where(at, lax.rem(node, 256).astype(F32), 0.0).astype(BF16)
    req[0] = dot_nt(onehot[...], reqb[...])

    for c in loads:
        c.wait()
    for c in range(6):
        for odd in range(2):
            value = dbuf[c, pl.ds(8 + odd, 64, stride=2), :] if c < 3 else vbuf[c - 3, pl.ds(odd, 64, stride=2), :]
            high, low = split(value)
            for t in range(4):
                rows = slice(t * 96 + c * 16, t * 96 + (c + 1) * 16)
                table[rows, odd * 128 : (odd + 1) * 128] = high[t * 16 : (t + 1) * 16]
                table[rows, 256 + odd * 128 : 256 + (odd + 1) * 128] = low[t * 16 : (t + 1) * 16]
    for c in range(3):
        turned = dbuf[c, 8:136, :].T
        colsend[0, c : c + 1, :] = turned[0:1, :]
        colsend[1, c : c + 1, :] = turned[127:128, :]
    loadb[192:256, :] = jnp.zeros((64, ENT), BF16)
    loadb[448:512, :] = jnp.zeros((64, ENT), BF16)
    force[...] = jnp.zeros((384, 256), F32)

    src, tgt = iota((NZ, NZ), 0), iota((NZ, NZ), 1)
    inner = stencil(src - tgt)
    ghost = jnp.where(src < 3, stencil(-(src + 1 + tgt)), 0.0)
    for i, (f, tab) in enumerate(((0, inner + ghost), (3, inner - ghost))):
        tab = tab.astype(BF16)
        tab = jnp.concatenate([tab, tab], axis=0)
        for b in range(4):
            high, low = split(xbuf[f, 3 + 8 * b : 11 + 8 * b].reshape(256, NZ))
            zb[i, b * 256 : (b + 1) * 256, :] = dot(jnp.concatenate([high, low], axis=1), tab)

    pl.semaphore_wait(barrier, ND - 1)

    def row(ref, at):
        return ref.at[:, pl.ds(at, 1)]

    def exchange(src, dst, index, recv):
        def send(s, c):
            pltpu.make_async_remote_copy(
                row(src, s * NC + c), row(dst, slot_row), sent.at[index], recv.at[mine],
                device_id=(s, c), device_id_type=MESH,
            ).start()

        each_peer(send)
        dst[:, pl.ds(slot_row, 1), :] = src[:, pl.ds(me, 1), :]

    def some(src, dst, count, send_sem, recv_sem):
        return pltpu.make_async_remote_copy(
            src.at[:, pl.ds(0, count)], dst.at[:, pl.ds(0, count)], send_sem, recv_sem,
            device_id=(span, chord), device_id_type=MESH,
        )

    def await_group(src, dst, index, recv, g):
        @pl.when(g == mine)
        def _():
            some(src, dst, 15, sent.at[index], recv.at[g]).wait_recv()

        @pl.when(g != mine)
        def _():
            some(src, dst, 16, sent.at[index], recv.at[g]).wait_recv()

    def near_first(k):
        half = (k + 1) // 2
        return lax.rem(mine + jnp.where(lax.rem(k, 2) == 1, half, 8 - half), 8)

    exchange(req, asked, 0, ask_r)

    up = (lax.rem(span + 1, NS), chord)
    down = (lax.rem(span + NS - 1, NS), chord)
    right = (span, lax.rem(chord + 1, NC))
    left = (span, lax.rem(chord + NC - 1, NC))
    moves = [
        (xbuf.at[:, pl.ds(CX, 3)], xbuf.at[:, pl.ds(0, 3)], up),
        (xbuf.at[:, pl.ds(3, 3)], xbuf.at[:, pl.ds(CX + 3, 3)], down),
        (ybuf.at[:, :, pl.ds(CY + 5, 3)], ybuf.at[:, :, pl.ds(5, 3)], right),
        (ybuf.at[:, :, pl.ds(8, 3)], ybuf.at[:, :, pl.ds(CY + 8, 3)], left),
        (dbuf.at[:, pl.ds(135, 1)], dbuf.at[:, pl.ds(7, 1)], up),
        (dbuf.at[:, pl.ds(8, 1)], dbuf.at[:, pl.ds(136, 1)], down),
        (colsend.at[1], collow, right),
        (colsend.at[0], colhigh, left),
    ]
    halos = [
        pltpu.make_async_remote_copy(a, b, halo_s.at[i], halo_r.at[i], device_id=to, device_id_type=MESH)
        for i, (a, b, to) in enumerate(moves)
    ]
    for h in halos:
        h.start()

    lane8 = iota((8, 128), 1)
    sub8 = iota((8, QW), 0)
    sub_y = iota((QW, QW), 0)

    def halves(ref, j, g):
        low = ref[j, pl.ds(pl.multiple_of(g * 8, 8), 8), :]
        high = ref[j, pl.ds(pl.multiple_of(g * 8 + 64, 8), 8), :]
        front = jnp.where(lane8 < 64, low, pltpu.roll(high, 64, 1))
        back = jnp.where(lane8 < 64, pltpu.roll(low, 64, 1), high)
        return front, back

    def pick(k, carry):
        g = near_first(k)
        await_group(req, asked, 0, ask_r, g)
        rows = pl.ds(pl.multiple_of(g * 8, 8), 8)
        xs, ys = halves(asked, 0, g)
        xs, ys = xs.astype(I32), ys.astype(I32)
        px[rows, :] = xs
        for t in range(4):
            yrow = jnp.concatenate([ys[2 * t : 2 * t + 1], ys[2 * t + 1 : 2 * t + 2]], axis=1)
            xrow = jnp.concatenate([xs[2 * t : 2 * t + 1], xs[2 * t + 1 : 2 * t + 2]], axis=1)
            hot = jnp.where(sub_y == yrow, 1.0, 0.0).astype(BF16)
            ohy[:, pl.ds(pl.multiple_of((g * 4 + t) * QW, QW), QW)] = hot
            out = dot(table[...], jnp.concatenate([hot, hot], axis=0))
            sums = [jnp.zeros((8, QW), F32) for _ in range(6)]
            for i in range(8):
                mask = sub8 + 8 * i == xrow
                for c in range(6):
                    at = (i // 2) * 96 + c * 16 + (i % 2) * 8
                    sums[c] = sums[c] + jnp.where(mask, out[at : at + 8], 0.0)
            for c in range(6):
                line = jnp.sum(sums[c], axis=0, keepdims=True)
                picked[c, 2 * t : 2 * t + 1, :] = line[:, 0:128]
                picked[c, 2 * t + 1 : 2 * t + 2, :] = line[:, 128:256]
        high_rows = pl.ds(pl.multiple_of(g * 8 + 64, 8), 8)
        for j in range(3):
            even, odd = picked[2 * j], picked[2 * j + 1]
            rep[j, rows, :] = jnp.where(lane8 < 64, even, pltpu.roll(odd, 64, 1))
            rep[j, high_rows, :] = jnp.where(lane8 < 64, pltpu.roll(even, 64, 1), odd)

        def reply(half, c):
            pltpu.make_async_remote_copy(
                row(rep, g * 8 + c + 64 * half), row(got, me), sent.at[1], reply_r,
                device_id=(2 * g + half, c), device_id_type=MESH,
            ).start()

        @pl.when(g != mine)
        def _():
            for half in range(2):
                for c in range(NC):
                    reply(half, c)

        @pl.when(g == mine)
        def _():
            for half in range(2):
                for c in range(NC):

                    @pl.when((2 * g + half != span) | (c != chord))
                    def _():
                        reply(half, c)

        return carry

    lax.fori_loop(0, 8, pick, 0)
    got[:, pl.ds(me, 1), :] = rep[:, pl.ds(slot_row, 1), :]

    for h in halos:
        h.wait_recv()

    @pl.when(span == 0)
    def _():
        xbuf[:, 0:3] = jnp.zeros((4, 3, CY, NZ), F32)
        dbuf[:, 7:8, :] = jnp.zeros((3, 1, 128), F32)

    @pl.when(span == NS - 1)
    def _():
        xbuf[:, CX + 3 : CX + 6] = jnp.zeros((4, 3, CY, NZ), F32)
        dbuf[:, 136:137, :] = jnp.zeros((3, 1, 128), F32)

    @pl.when(chord == 0)
    def _():
        ybuf[:, :, 5:8, :] = jnp.zeros((2, CX, 3, NZ), F32)
        collow[...] = jnp.zeros((8, 128), F32)

    @pl.when(chord == NC - 1)
    def _():
        ybuf[:, :, CY + 8 : CY + 11, :] = jnp.zeros((2, CX, 3, NZ), F32)
        colhigh[...] = jnp.zeros((8, 128), F32)

    def plane(x, carry):
        def dx(f):
            return diff(*[xbuf[f, x + 3 + o] for o in (3, 2, 1, -1, -2, -3)])

        def dy(f):
            return diff(*[ybuf[f, x, 8 + o : 8 + CY + o, :] for o in (3, 2, 1, -1, -2, -3)])

        zrows = pl.ds(pl.multiple_of(x * CY, CY), CY)
        dp, du = dx(0), dx(1)
        fo[0, x] = xbuf[0, x + 3] - SCALE * (0.5 * dp + du + dy(1) + zb[1, zrows, :])
        fo[1, x] = xbuf[1, x + 3] - SCALE * (0.5 * du + dp)
        fo[2, x] = xbuf[2, x + 3] - SCALE * (0.5 * dx(2) + dy(0))
        fo[3, x] = xbuf[3, x + 3] - SCALE * (0.5 * dx(3) + zb[0, zrows, :])
        return carry

    lax.fori_loop(0, CX, plane, 0)
    for b in range(8):
        turned = fo[0, 4 * b : 4 * b + 4].reshape(128, NZ).T
        p0[0:1, b * 128 : (b + 1) * 128] = turned[0:1, :]

    def columns(g, carry):
        rows = pl.ds(pl.multiple_of(g * 8, 8), 8)
        xs = px[rows, :]
        for t in range(8):
            hot = jnp.where(sub_s[:, 0:128] == xs[t : t + 1], 1.0, 0.0).astype(BF16)
            ohx[:, pl.ds(pl.multiple_of((g * 8 + t) * 128, 128), 128)] = hot
        return carry

    lax.fori_loop(0, 8, columns, 0)

    some(rep, got, ND - 1, sent.at[1], reply_r).wait_recv()
    for j in range(3):
        high, low = split(got[j].T)
        lookup[j * 128 : (j + 1) * 128, 0:128] = high
        lookup[j * 128 : (j + 1) * 128, 128:256] = low

    def interp(q, carry):
        cols = pl.ds(pl.multiple_of(q * QW, QW), QW)
        totals = [jnp.zeros((8, QW), F32) for _ in range(6)]
        for k in range(K):
            hot = onehot[:, pl.ds(pl.multiple_of(k * PTS + q * QW, QW), QW)]
            out = dot(lookup[...], jnp.concatenate([hot, hot], axis=0))
            at = sub_s == rank[k : k + 1, cols]
            weight = w_ref[k : k + 1, cols]
            for c in range(6):
                part = jnp.where(at, out[c * CAP : (c + 1) * CAP], 0.0)
                totals[c] = totals[c] + weight * jnp.sum(part.reshape(8, 8, QW), axis=0)
        for c in range(6):
            motion_ref[c : c + 1, cols] = jnp.sum(totals[c], axis=0, keepdims=True)
        return carry

    lax.fori_loop(0, PTS // QW, interp, 0)

    pressure = p0[0:1, :] + (SCALE * 74.0) * motion_ref[5:6, :]
    for q in range(PTS // QW):
        cols = slice(q * QW, (q + 1) * QW)
        for k in range(K):
            ent = slice(k * PTS + q * QW, k * PTS + (q + 1) * QW)
            at = sub_s == rank[k : k + 1, cols]
            for c in range(3):
                value = nrm_ref[c : c + 1, cols] * pressure[:, cols] * w_ref[k : k + 1, cols]
                high = value.astype(BF16).astype(F32)
                loadb[c * CAP : (c + 1) * CAP, ent] = jnp.where(at, high, 0.0).astype(BF16)
                loadb[256 + c * CAP : 256 + (c + 1) * CAP, ent] = jnp.where(at, value - high, 0.0).astype(BF16)
    both = dot_nt(onehot[...], loadb[...])
    outg[0] = both[:, 0:128] + both[:, 256:384]
    outg[1] = both[:, 128:256] + both[:, 384:512]
    exchange(outg, arrived, 2, load_r)

    zlane = iota((128, NZ), 1)
    reach = jnp.where(zlane == 0, 74.0 * SCALE, jnp.where(zlane == 1, -16.0 * SCALE, jnp.where(zlane == 2, 2.0 * SCALE, 0.0)))
    for b in range(8):
        turned = jnp.broadcast_to(motion_ref[5:6, b * 128 : (b + 1) * 128], (8, 128)).T
        fix = (turned[:, 0:1] * reach).reshape(4, CY, NZ)
        fo[0, 4 * b : 4 * b + 4] = fo[0, 4 * b : 4 * b + 4] + fix

    def collect(k, carry):
        g = near_first(k)
        await_group(outg, arrived, 2, load_r, g)
        cols = pl.ds(pl.multiple_of(g * 1024, 1024), 1024)
        values = halves(arrived, 0, g) + halves(arrived, 1, g)[0:1]
        for c in range(3):
            high = values[c].astype(BF16).astype(F32)
            for half, value in enumerate((high, values[c] - high)):
                for t in range(8):
                    wide = jnp.broadcast_to(value[t : t + 1], (16, 128)).astype(BF16)
                    wide = jnp.concatenate([wide] * 4, axis=0)
                    hot = ohx[:, pl.ds(pl.multiple_of((g * 8 + t) * 128, 128), 128)]
                    at = (half * 3 + c) * 64
                    fb[at : at + 64, t * 128 : (t + 1) * 128] = hot * wide
        force[...] += dot_nt(fb[...], ohy[:, cols])
        return carry

    lax.fori_loop(0, 8, collect, 0)
    for c in range(3):
        total = force[c * 64 : (c + 1) * 64, :] + force[192 + c * 64 : 192 + (c + 1) * 64, :]
        spread[c, pl.ds(0, 64, stride=2), :] = total[:, 0:128]
        spread[c, pl.ds(1, 64, stride=2), :] = total[:, 128:256]

    lane128 = iota((128, 128), 1)
    low_t, high_t = collow[...].T, colhigh[...].T
    for c in range(3):
        mid = dbuf[c, 8:136, :]
        west = jnp.where(lane128 == 0, low_t[:, c : c + 1], pltpu.roll(mid, 1, 1))
        east = jnp.where(lane128 == 127, high_t[:, c : c + 1], pltpu.roll(mid, 127, 1))
        lap = dbuf[c, 9:137, :] + dbuf[c, 7:135, :] + east + west - 4.0 * mid
        vel = vbuf[c]
        vel_new = vel + 0.3 * (0.5 * lap + spread[c] - 0.2 * vel)
        vel_out[c] = vel_new
        disp_out[c] = mid + 0.3 * vel_new

    for h in halos:
        h.wait_send()
    for index, (src, dst) in enumerate(((req, asked), (rep, got), (outg, arrived))):
        some(src, dst, ND - 1, sent.at[index], reply_r).wait_send()


def put(fo, motion, disp, vel, fo_out, motion_out, disp_out, vel_out, sems):
    pairs = [(fo.at[i], fo_out.at[i]) for i in range(4)] + [(motion, motion_out), (disp, disp_out), (vel, vel_out)]
    copies = [pltpu.make_async_copy(a, b, sems.at[i]) for i, (a, b) in enumerate(pairs)]
    for c in copies:
        c.start()
    for c in copies:
        c.wait()


def body(fluid, disp, vel, owners, nodes, weights, normals):
    small = pl.BlockSpec(memory_space=pltpu.VMEM)
    big = pl.BlockSpec(memory_space=pltpu.HBM)
    vm = pltpu.VMEM
    dma = pltpu.SemaphoreType.DMA
    scratch = [
        vm((4, CX + 6, CY, NZ), F32),
        vm((2, CX, CY + 16, NZ), F32),
        vm((2, PTS, NZ), F32),
        vm((3, 144, 128), F32),
        vm((3, 128, 128), F32),
        vm((ND, ENT), BF16),
        vm((K, PTS), I32),
        vm((128, ENT), BF16),
        vm((1, ND, 128), F32),
        vm((1, ND, 128), F32),
        vm((CAP, 128), I32),
        vm((384, 512), BF16),
        vm((256, SLOTS), BF16),
        vm((64, SLOTS), BF16),
        vm((6, 8, 128), F32),
        vm((3, ND, 128), F32),
        vm((3, ND, 128), F32),
        vm((384, 256), BF16),
        vm((8, PTS), F32),
        vm((512, ENT), BF16),
        vm((2, ND, 128), F32),
        vm((2, ND, 128), F32),
        vm((384, 1024), BF16),
        vm((384, 256), F32),
        vm((3, 128, 128), F32),
        vm((2, 8, 128), F32),
        vm((8, 128), F32),
        vm((8, 128), F32),
        dma((5,)),
        dma((8,)),
        dma((8,)),
        dma((3,)),
        dma((8,)),
        dma(()),
        dma((8,)),
    ]
    shapes = (fluid.shape, (6, PTS), disp.shape, vel.shape)
    done = pl.pallas_call(
        kernel,
        name="coupling",
        out_shape=tuple(vm(shape, F32) for shape in shapes),
        in_specs=[small] * 4 + [big] * 3,
        out_specs=(small,) * 4,
        scratch_shapes=scratch,
        compiler_params=pltpu.CompilerParams(
            collective_id=0, has_side_effects=True, vmem_limit_bytes=64_400_000
        ),
    )(owners.T, nodes.T, weights.T, normals, fluid, disp, vel)
    return pl.pallas_call(
        put,
        name="put",
        out_shape=tuple(jax.ShapeDtypeStruct(shape, F32) for shape in shapes),
        in_specs=[small] * 4,
        out_specs=(big,) * 4,
        scratch_shapes=[dma((7,))],
        compiler_params=pltpu.CompilerParams(vmem_limit_bytes=1024 * 1024),
    )(*[pltpu.with_memory_space_constraint(part, pltpu.VMEM) for part in done])


def solution(mesh):
    block, line = P(None, "span", "chord"), P(("span", "chord"), None)
    return jax.shard_map(
        body,
        mesh=mesh,
        in_specs=(P(None, "span", "chord", None), block, block, line, line, line, P(None, ("span", "chord"))),
        out_specs=(P(None, "span", "chord", None), P(None, ("span", "chord")), block, block),
        check_vma=False,
    )
```

time: 55.7 us -> 44.5 us (0.80)
  Pallas kernels: 49.7 us -> 43.6 us
  local copies, waits for them, and re-layouts: 5.11 us -> 0 us
    pallas_call x1 -> x2, Pallas kernels: 49.7 us -> 43.6 us  [the longest x1 42.1 us: body(): pl.pallas_call(kernel, name='coupling', out_shape=tuple((vm(shape, F32) f...]
    unnamed x10 -> x0, local copies, waits for them, and re-layouts: 5.11 us -> none
where the time goes in v2:
time: 44.5 us; the launch traced here: 44.2 us
  Pallas kernels  43.6 us (98%)
  between operations  0.64 us (1%)
    pallas_call x1, Pallas kernels, body(): pl.pallas_call(kernel, name='coupling', out_shape=tuple((vm(shape, F32) f...  42.1 us
    pallas_call x1, Pallas kernels, body(): pl.pallas_call(put, name='put', out_shape=tuple((jax.ShapeDtypeStruct(sha...  1.51 us

profile of v2, /device:TPU:1, one launch (start us, length us, event | category | flops | bytes accessed | tf_op | source)
XLA Modules:
  0.0 44.2 jit_solution(11743241562219422292)
XLA Ops:
  0.6 42.1 %coupling.1 = (f32[4,32,32,128]{3,2,1,0:T(8,128)S(1)}, f32[6,1024]{1,0:T(8,128)S(1)}, f32[3,128,128]{2,1,0:T(8,128)S(1)}, f32[3,128,128]{2,1,0:T(8,128)S(1)}) custom-call(s32[4,1024]{1,0:T(4,128)} %bitcast.3, s32[4,1024]{1,0:T(4,128)} %bitcast.4, f32[4,1024]{1,0:T(4,128)} %bitcast.5, f32[3,1024]{1,0:T(4,128)} %nrm_ref.1, f32[4,32,32,128]{3,2,1,0:T(8,128)} %fluid_hbm.1, ...), custom_call_target="tpu_custom_call" | custom-call | tf_op jit(solution)/shard_map/coupling/pallas_call | solution.py:470
  42.7 1.5 %put.1 = (f32[4,32,32,128]{3,2,1,0:T(8,128)}, f32[6,1024]{1,0:T(8,128)}, f32[3,128,128]{2,1,0:T(8,128)}, f32[3,128,128]{2,1,0:T(8,128)}) custom-call(f32[4,32,32,128]{3,2,1,0:T(8,128)S(1)} %get-tuple-element.8.fo, f32[6,1024]{1,0:T(8,128)S(1)} %get-tuple-element.9.motion, f32[3,128,128]{2,1,0:T(8,128)S(1)} %get-tuple-element.10.disp, ...), custom_call_target="tpu_custom_call" | custom-call | tf_op jit(solution)/shard_map/put/pallas_call | solution.py:481

commit v3 on v2

--- a/solution.py
+++ b/solution.py
@@ -47,11 +47,11 @@
 
 def kernel(
     own_ref, node_ref, w_ref, nrm_ref, fluid_hbm, disp_hbm, vel_hbm,
-    fo, motion_ref, disp_out, vel_out,
+    fo, motion_ref, disp_ref, base_ref, force,
     xbuf, ybuf, zb, dbuf, vbuf,
-    onehot, rank, reqb, req, asked, px,
+    onehot, rank, rankhot, reqb, req, asked, px,
     table, ohy, ohx, picked, rep, got, lookup, p0,
-    loadb, outg, arrived, fb, force, spread, colsend, collow, colhigh,
+    loadb, outg, arrived, fb, colsend, collow, colhigh,
     in_sem, halo_s, halo_r, sent, ask_r, reply_r, load_r,
 ):
     span, chord = lax.axis_index("span"), lax.axis_index("chord")
@@ -116,12 +116,13 @@
         offset = offset + dot(count, ones)
         for k in range(K):
             slot = jnp.sum(jnp.where(masks[k], prior, 0.0), axis=0, keepdims=True).astype(I32)
-            rank[k : k + 1, cols] = slot
             node = node_ref[k : k + 1, cols]
+            ent = slice(k * PTS + q * QW, k * PTS + (q + 1) * QW)
             at = sub_s == slot
-            ent = slice(k * PTS + q * QW, k * PTS + (q + 1) * QW)
+            rankhot[:, ent] = jnp.where(at, 1.0, 0.0).astype(BF16)
             reqb[0:CAP, ent] = jnp.where(at, (node // 256).astype(F32), 0.0).astype(BF16)
             reqb[CAP:, ent] = jnp.where(at, lax.rem(node, 256).astype(F32), 0.0).astype(BF16)
+            rank[k : k + 1, cols] = slot
     req[0] = dot_nt(onehot[...], reqb[...])
 
     for c in loads:
@@ -138,8 +139,6 @@
         turned = dbuf[c, 8:136, :].T
         colsend[0, c : c + 1, :] = turned[0:1, :]
         colsend[1, c : c + 1, :] = turned[127:128, :]
-    loadb[192:256, :] = jnp.zeros((64, ENT), BF16)
-    loadb[448:512, :] = jnp.zeros((64, ENT), BF16)
     force[...] = jnp.zeros((384, 256), F32)
 
     src, tgt = iota((NZ, NZ), 0), iota((NZ, NZ), 1)
@@ -185,6 +184,10 @@
     def near_first(k):
         half = (k + 1) // 2
         return lax.rem(mine + jnp.where(lax.rem(k, 2) == 1, half, 8 - half), 8)
+
+    def round_trip(k):
+        step = jnp.where(k < 2, k, jnp.where(k < 4, k + 2, jnp.where(k == 4, 3, jnp.where(k == 5, 6, 2))))
+        return lax.rem(mine + jnp.where(k == 7, 7, step), 8)
 
     exchange(req, asked, 0, ask_r)
 
@@ -210,8 +213,17 @@
         h.start()
 
     lane8 = iota((8, 128), 1)
-    sub8 = iota((8, QW), 0)
-    sub_y = iota((QW, QW), 0)
+    sub8f = iota((8, QW), 0).astype(F32)
+    low_y = iota((256, QW), 0).astype(F32).astype(BF16)
+    low_x = iota((64, 128), 0).astype(F32).astype(BF16)
+    one, zero = jnp.ones((), BF16), jnp.zeros((), BF16)
+
+    def tall(line, rows):
+        wide = jnp.broadcast_to(line, (16, line.shape[1])).astype(BF16)
+        return jnp.concatenate([wide] * (rows // 16), axis=0)
+
+    def hot_rows(numbers, line, rows):
+        return jnp.where(numbers == tall(line, rows), one, zero)
 
     def halves(ref, j, g):
         low = ref[j, pl.ds(pl.multiple_of(g * 8, 8), 8), :]
@@ -221,21 +233,22 @@
         return front, back
 
     def pick(k, carry):
-        g = near_first(k)
+        g = round_trip(k)
         await_group(req, asked, 0, ask_r, g)
         rows = pl.ds(pl.multiple_of(g * 8, 8), 8)
         xs, ys = halves(asked, 0, g)
-        xs, ys = xs.astype(I32), ys.astype(I32)
         px[rows, :] = xs
+        group = [pl.ds(pl.multiple_of((g * 4 + t) * QW, QW), QW) for t in range(4)]
         for t in range(4):
             yrow = jnp.concatenate([ys[2 * t : 2 * t + 1], ys[2 * t + 1 : 2 * t + 2]], axis=1)
+            ohy[:, group[t]] = hot_rows(low_y, yrow, 256)
+        for t in range(4):
             xrow = jnp.concatenate([xs[2 * t : 2 * t + 1], xs[2 * t + 1 : 2 * t + 2]], axis=1)
-            hot = jnp.where(sub_y == yrow, 1.0, 0.0).astype(BF16)
-            ohy[:, pl.ds(pl.multiple_of((g * 4 + t) * QW, QW), QW)] = hot
+            hot = ohy[:, group[t]]
             out = dot(table[...], jnp.concatenate([hot, hot], axis=0))
             sums = [jnp.zeros((8, QW), F32) for _ in range(6)]
             for i in range(8):
-                mask = sub8 + 8 * i == xrow
+                mask = sub8f + 8.0 * i == xrow
                 for c in range(6):
                     at = (i // 2) * 96 + c * 16 + (i % 2) * 8
                     sums[c] = sums[c] + jnp.where(mask, out[at : at + 8], 0.0)
@@ -322,8 +335,7 @@
         rows = pl.ds(pl.multiple_of(g * 8, 8), 8)
         xs = px[rows, :]
         for t in range(8):
-            hot = jnp.where(sub_s[:, 0:128] == xs[t : t + 1], 1.0, 0.0).astype(BF16)
-            ohx[:, pl.ds(pl.multiple_of((g * 8 + t) * 128, 128), 128)] = hot
+            ohx[:, pl.ds(pl.multiple_of((g * 8 + t) * 128, 128), 128)] = hot_rows(low_x, xs[t : t + 1], 64)
         return carry
 
     lax.fori_loop(0, 8, columns, 0)
@@ -331,8 +343,13 @@
     some(rep, got, ND - 1, sent.at[1], reply_r).wait_recv()
     for j in range(3):
         high, low = split(got[j].T)
-        lookup[j * 128 : (j + 1) * 128, 0:128] = high
-        lookup[j * 128 : (j + 1) * 128, 128:256] = low
+        for c in range(2):
+            for t in range(4):
+                at = t * 96 + (2 * j + c) * 16
+                lookup[at : at + 16, 0:128] = high[c * 64 + t * 16 : c * 64 + (t + 1) * 16]
+                lookup[at : at + 16, 128:256] = low[c * 64 + t * 16 : c * 64 + (t + 1) * 16]
+
+    sub8i = iota((8, QW), 0)
 
     def interp(q, carry):
         cols = pl.ds(pl.multiple_of(q * QW, QW), QW)
@@ -340,11 +357,16 @@
         for k in range(K):
             hot = onehot[:, pl.ds(pl.multiple_of(k * PTS + q * QW, QW), QW)]
             out = dot(lookup[...], jnp.concatenate([hot, hot], axis=0))
-            at = sub_s == rank[k : k + 1, cols]
+            slot = rank[k : k + 1, cols]
             weight = w_ref[k : k + 1, cols]
+            sums = [jnp.zeros((8, QW), F32) for _ in range(6)]
+            for i in range(8):
+                mask = sub8i + 8 * i == slot
+                for c in range(6):
+                    at = (i // 2) * 96 + c * 16 + (i % 2) * 8
+                    sums[c] = sums[c] + jnp.where(mask, out[at : at + 8], 0.0)
             for c in range(6):
-                part = jnp.where(at, out[c * CAP : (c + 1) * CAP], 0.0)
-                totals[c] = totals[c] + weight * jnp.sum(part.reshape(8, 8, QW), axis=0)
+                totals[c] = totals[c] + weight * sums[c]
         for c in range(6):
             motion_ref[c : c + 1, cols] = jnp.sum(totals[c], axis=0, keepdims=True)
         return carry
@@ -352,19 +374,19 @@
     lax.fori_loop(0, PTS // QW, interp, 0)
 
     pressure = p0[0:1, :] + (SCALE * 74.0) * motion_ref[5:6, :]
-    for q in range(PTS // QW):
-        cols = slice(q * QW, (q + 1) * QW)
-        for k in range(K):
-            ent = slice(k * PTS + q * QW, k * PTS + (q + 1) * QW)
-            at = sub_s == rank[k : k + 1, cols]
-            for c in range(3):
-                value = nrm_ref[c : c + 1, cols] * pressure[:, cols] * w_ref[k : k + 1, cols]
-                high = value.astype(BF16).astype(F32)
-                loadb[c * CAP : (c + 1) * CAP, ent] = jnp.where(at, high, 0.0).astype(BF16)
-                loadb[256 + c * CAP : 256 + (c + 1) * CAP, ent] = jnp.where(at, value - high, 0.0).astype(BF16)
-    both = dot_nt(onehot[...], loadb[...])
-    outg[0] = both[:, 0:128] + both[:, 256:384]
-    outg[1] = both[:, 128:256] + both[:, 384:512]
+    both = jnp.zeros((ND, 384), F32)
+    push = [nrm_ref[c : c + 1, :] * pressure for c in range(3)]
+    for k in range(K):
+        ent = slice(k * PTS, (k + 1) * PTS)
+        for c in range(3):
+            value = push[c] * w_ref[k : k + 1, :]
+            high = value.astype(BF16).astype(F32)
+            for half, part in enumerate((high, value - high)):
+                at = (c + 2 * half) * CAP if c < 2 else (4 + half) * CAP
+                loadb[at : at + CAP, ent] = rankhot[:, ent] * tall(part, CAP)
+        both = both + dot_nt(onehot[:, ent], loadb[:, ent])
+    outg[0] = both[:, 0:128] + both[:, 128:256]
+    outg[1] = both[:, 256:384] + pltpu.roll(both[:, 256:384], 64, 1)
     exchange(outg, arrived, 2, load_r)
 
     zlane = iota((128, NZ), 1)
@@ -373,6 +395,17 @@
         turned = jnp.broadcast_to(motion_ref[5:6, b * 128 : (b + 1) * 128], (8, 128)).T
         fix = (turned[:, 0:1] * reach).reshape(4, CY, NZ)
         fo[0, 4 * b : 4 * b + 4] = fo[0, 4 * b : 4 * b + 4] + fix
+
+    lane128 = iota((128, 128), 1)
+    low_t, high_t = collow[...].T, colhigh[...].T
+    for c in range(3):
+        mid = dbuf[c, 8:136, :]
+        west = jnp.where(lane128 == 0, low_t[:, c : c + 1], pltpu.roll(mid, 1, 1))
+        east = jnp.where(lane128 == 127, high_t[:, c : c + 1], pltpu.roll(mid, 127, 1))
+        lap = dbuf[c, 9:137, :] + dbuf[c, 7:135, :] + east + west - 4.0 * mid
+        vel = vbuf[c]
+        base_ref[c] = vel + 0.3 * (0.5 * lap - 0.2 * vel)
+        disp_ref[c] = mid
 
     def collect(k, carry):
         g = near_first(k)
@@ -383,42 +416,32 @@
             high = values[c].astype(BF16).astype(F32)
             for half, value in enumerate((high, values[c] - high)):
                 for t in range(8):
-                    wide = jnp.broadcast_to(value[t : t + 1], (16, 128)).astype(BF16)
-                    wide = jnp.concatenate([wide] * 4, axis=0)
                     hot = ohx[:, pl.ds(pl.multiple_of((g * 8 + t) * 128, 128), 128)]
                     at = (half * 3 + c) * 64
-                    fb[at : at + 64, t * 128 : (t + 1) * 128] = hot * wide
+                    fb[at : at + 64, t * 128 : (t + 1) * 128] = hot * tall(value[t : t + 1], 64)
         force[...] += dot_nt(fb[...], ohy[:, cols])
         return carry
 
     lax.fori_loop(0, 8, collect, 0)
-    for c in range(3):
-        total = force[c * 64 : (c + 1) * 64, :] + force[192 + c * 64 : 192 + (c + 1) * 64, :]
-        spread[c, pl.ds(0, 64, stride=2), :] = total[:, 0:128]
-        spread[c, pl.ds(1, 64, stride=2), :] = total[:, 128:256]
-
-    lane128 = iota((128, 128), 1)
-    low_t, high_t = collow[...].T, colhigh[...].T
-    for c in range(3):
-        mid = dbuf[c, 8:136, :]
-        west = jnp.where(lane128 == 0, low_t[:, c : c + 1], pltpu.roll(mid, 1, 1))
-        east = jnp.where(lane128 == 127, high_t[:, c : c + 1], pltpu.roll(mid, 127, 1))
-        lap = dbuf[c, 9:137, :] + dbuf[c, 7:135, :] + east + west - 4.0 * mid
-        vel = vbuf[c]
-        vel_new = vel + 0.3 * (0.5 * lap + spread[c] - 0.2 * vel)
-        vel_out[c] = vel_new
-        disp_out[c] = mid + 0.3 * vel_new
-
     for h in halos:
         h.wait_send()
     for index, (src, dst) in enumerate(((req, asked), (rep, got), (outg, arrived))):
         some(src, dst, ND - 1, sent.at[index], reply_r).wait_send()
 
 
-def put(fo, motion, disp, vel, fo_out, motion_out, disp_out, vel_out, sems):
-    pairs = [(fo.at[i], fo_out.at[i]) for i in range(4)] + [(motion, motion_out), (disp, disp_out), (vel, vel_out)]
+def finish(fo, motion, disp, base, force, fo_out, motion_out, disp_out, vel_out, disp_new, vel_new, sems):
+    pairs = [(fo.at[i], fo_out.at[i]) for i in range(4)] + [(motion, motion_out), (disp_new, disp_out), (vel_new, vel_out)]
     copies = [pltpu.make_async_copy(a, b, sems.at[i]) for i, (a, b) in enumerate(pairs)]
-    for c in copies:
+    for c in copies[:5]:
+        c.start()
+    for c in range(3):
+        total = force[c * 64 : (c + 1) * 64, :] + force[192 + c * 64 : 192 + (c + 1) * 64, :]
+        for odd in range(2):
+            rows = pl.ds(odd, 64, stride=2)
+            vel = base[c, rows, :] + 0.3 * total[:, odd * 128 : (odd + 1) * 128]
+            vel_new[c, rows, :] = vel
+            disp_new[c, rows, :] = disp[c, rows, :] + 0.3 * vel
+    for c in copies[5:]:
         c.start()
     for c in copies:
         c.wait()
@@ -437,10 +460,11 @@
         vm((3, 128, 128), F32),
         vm((ND, ENT), BF16),
         vm((K, PTS), I32),
+        vm((CAP, ENT), BF16),
         vm((128, ENT), BF16),
         vm((1, ND, 128), F32),
         vm((1, ND, 128), F32),
-        vm((CAP, 128), I32),
+        vm((CAP, 128), F32),
         vm((384, 512), BF16),
         vm((256, SLOTS), BF16),
         vm((64, SLOTS), BF16),
@@ -449,12 +473,10 @@
         vm((3, ND, 128), F32),
         vm((384, 256), BF16),
         vm((8, PTS), F32),
-        vm((512, ENT), BF16),
+        vm((384, ENT), BF16),
         vm((2, ND, 128), F32),
         vm((2, ND, 128), F32),
         vm((384, 1024), BF16),
-        vm((384, 256), F32),
-        vm((3, 128, 128), F32),
         vm((2, 8, 128), F32),
         vm((8, 128), F32),
         vm((8, 128), F32),
@@ -467,24 +489,25 @@
         dma((8,)),
     ]
     shapes = (fluid.shape, (6, PTS), disp.shape, vel.shape)
+    kept = shapes + ((384, 256),)
     done = pl.pallas_call(
         kernel,
         name="coupling",
-        out_shape=tuple(vm(shape, F32) for shape in shapes),
+        out_shape=tuple(vm(shape, F32) for shape in kept),
         in_specs=[small] * 4 + [big] * 3,
-        out_specs=(small,) * 4,
+        out_specs=(small,) * 5,
         scratch_shapes=scratch,
         compiler_params=pltpu.CompilerParams(
-            collective_id=0, has_side_effects=True, vmem_limit_bytes=64_400_000
+            collective_id=0, has_side_effects=True, vmem_limit_bytes=64_000_000
         ),
     )(owners.T, nodes.T, weights.T, normals, fluid, disp, vel)
     return pl.pallas_call(
-        put,
-        name="put",
+        finish,
+        name="finish",
         out_shape=tuple(jax.ShapeDtypeStruct(shape, F32) for shape in shapes),
-        in_specs=[small] * 4,
+        in_specs=[small] * 5,
         out_specs=(big,) * 4,
-        scratch_shapes=[dma((7,))],
+        scratch_shapes=[vm(disp.shape, F32), vm(vel.shape, F32), dma((7,))],
         compiler_params=pltpu.CompilerParams(vmem_limit_bytes=1024 * 1024),
     )(*[pltpu.with_memory_space_constraint(part, pltpu.VMEM) for part in done])
 

time: 44.5 us -> 44.1 us (level)
  no operation moved by 1% of the time
where the time goes in v3:
time: 44.1 us; the launch traced here: 43.8 us
  Pallas kernels  43.2 us (98%)
  between operations  0.64 us (1%)
    pallas_call x1, Pallas kernels, body(): pl.pallas_call(kernel, name='coupling', out_shape=tuple((vm(shape, F32) f...  41.7 us
    pallas_call x1, Pallas kernels, body(): pl.pallas_call(finish, name='finish', out_shape=tuple((jax.ShapeDtypeStru...  1.51 us

profile of v3, /device:TPU:1, one launch (start us, length us, event | category | flops | bytes accessed | tf_op | source)
XLA Modules:
  0.0 43.8 jit_solution(7487006954008294451)
XLA Ops:
  0.6 41.7 %coupling.1 = (f32[4,32,32,128]{3,2,1,0:T(8,128)S(1)}, f32[6,1024]{1,0:T(8,128)S(1)}, f32[3,128,128]{2,1,0:T(8,128)S(1)}, f32[3,128,128]{2,1,0:T(8,128)S(1)}, f32[384,256]{1,0:T(8,128)S(1)}) custom-call(s32[4,1024]{1,0:T(4,128)} %bitcast.3, s32[4,1024]{1,0:T(4,128)} %bitcast.4, f32[4,1024]{1,0:T(4,128)} %bitcast.5, f32[3,1024]{1,0:T(4,128)} %nrm_ref.1, ...), custom_call_target="tpu_custom_call" | custom-call | tf_op jit(solution)/shard_map/coupling/pallas_call | solution.py:493
  42.3 1.5 %finish.1 = (f32[4,32,32,128]{3,2,1,0:T(8,128)}, f32[6,1024]{1,0:T(8,128)}, f32[3,128,128]{2,1,0:T(8,128)}, f32[3,128,128]{2,1,0:T(8,128)}) custom-call(f32[4,32,32,128]{3,2,1,0:T(8,128)S(1)} %get-tuple-element.9.fo, f32[6,1024]{1,0:T(8,128)S(1)} %get-tuple-element.10.motion, f32[3,128,128]{2,1,0:T(8,128)S(1)} %get-tuple-element.11.disp, ...), custom_call_target="tpu_custom_call" | custom-call | tf_op jit(solution)/shard_map/finish/pallas_call | solution.py:504

commit v4 on v3

--- a/solution.py
+++ b/solution.py
@@ -72,13 +72,15 @@
 
     barrier = pltpu.get_barrier_semaphore()
 
-    def far_first(k):
-        half = (k + 1) // 2
-        return lax.rem(span + 10 + jnp.where(lax.rem(k, 2) == 1, half, 16 - half), NS)
-
-    def each_peer(act):
+    def late_first(k, across):
+        a, b = k // 4, lax.rem(k, 4)
+        z = jnp.where(a < 2, 2 + a, 3 - a) if across == 4 else 1 - a
+        x = jnp.where(b == 0, 2, jnp.where(b == 3, 0, 2 * b - 1))
+        return x * across + z
+
+    def each_peer(act, backward=False):
         def one(k, carry):
-            s = far_first(k)
+            s = late_first(NS - 1 - k if backward else k, 4)
 
             @pl.when(s != span)
             def _():
@@ -94,7 +96,7 @@
             def _():
                 act(span, c)
 
-    each_peer(lambda s, c: pl.semaphore_signal(barrier, 1, device_id=(s, c), device_id_type=MESH))
+    each_peer(lambda s, c: pl.semaphore_signal(barrier, 1, device_id=(s, c), device_id_type=MESH), True)
 
     before = (iota((QW, QW), 0) < iota((QW, QW), 1)).astype(F32).astype(BF16)
     ones = jnp.ones((QW, QW), BF16)
@@ -181,14 +183,6 @@
         def _():
             some(src, dst, 16, sent.at[index], recv.at[g]).wait_recv()
 
-    def near_first(k):
-        half = (k + 1) // 2
-        return lax.rem(mine + jnp.where(lax.rem(k, 2) == 1, half, 8 - half), 8)
-
-    def round_trip(k):
-        step = jnp.where(k < 2, k, jnp.where(k < 4, k + 2, jnp.where(k == 4, 3, jnp.where(k == 5, 6, 2))))
-        return lax.rem(mine + jnp.where(k == 7, 7, step), 8)
-
     exchange(req, asked, 0, ask_r)
 
     up = (lax.rem(span + 1, NS), chord)
@@ -233,7 +227,7 @@
         return front, back
 
     def pick(k, carry):
-        g = round_trip(k)
+        g = late_first(k, 2)
         await_group(req, asked, 0, ask_r, g)
         rows = pl.ds(pl.multiple_of(g * 8, 8), 8)
         xs, ys = halves(asked, 0, g)
@@ -408,7 +402,7 @@
         disp_ref[c] = mid
 
     def collect(k, carry):
-        g = near_first(k)
+        g = late_first(k, 2)
         await_group(outg, arrived, 2, load_r, g)
         cols = pl.ds(pl.multiple_of(g * 1024, 1024), 1024)
         values = halves(arrived, 0, g) + halves(arrived, 1, g)[0:1]

time: 44.1 us -> 41.6 us (0.943)
  Pallas kernels: 43.2 us -> 40.7 us
    pallas_call x1, Pallas kernels: 41.7 us -> 39.2 us  [body(): pl.pallas_call(kernel, name='coupling', out_shape=tuple((vm(shape, F32) f...]
where the time goes in v4:
time: 41.6 us; the launch traced here: 41.3 us
  Pallas kernels  40.7 us (98%)
  between operations  0.64 us (2%)
    pallas_call x1, Pallas kernels, body(): pl.pallas_call(kernel, name='coupling', out_shape=tuple((vm(shape, F32) f...  39.2 us
    pallas_call x1, Pallas kernels, body(): pl.pallas_call(finish, name='finish', out_shape=tuple((jax.ShapeDtypeStru...  1.51 us

profile of v4, /device:TPU:1, one launch (start us, length us, event | category | flops | bytes accessed | tf_op | source)
XLA Modules:
  0.0 41.3 jit_solution(16086054468874413290)
XLA Ops:
  0.6 39.2 %coupling.1 = (f32[4,32,32,128]{3,2,1,0:T(8,128)S(1)}, f32[6,1024]{1,0:T(8,128)S(1)}, f32[3,128,128]{2,1,0:T(8,128)S(1)}, f32[3,128,128]{2,1,0:T(8,128)S(1)}, f32[384,256]{1,0:T(8,128)S(1)}) custom-call(s32[4,1024]{1,0:T(4,128)} %bitcast.3, s32[4,1024]{1,0:T(4,128)} %bitcast.4, f32[4,1024]{1,0:T(4,128)} %bitcast.5, f32[3,1024]{1,0:T(4,128)} %nrm_ref.1, ...), custom_call_target="tpu_custom_call" | custom-call | tf_op jit(solution)/shard_map/coupling/pallas_call | solution.py:487
  39.8 1.5 %finish.1 = (f32[4,32,32,128]{3,2,1,0:T(8,128)}, f32[6,1024]{1,0:T(8,128)}, f32[3,128,128]{2,1,0:T(8,128)}, f32[3,128,128]{2,1,0:T(8,128)}) custom-call(f32[4,32,32,128]{3,2,1,0:T(8,128)S(1)} %get-tuple-element.9.fo, f32[6,1024]{1,0:T(8,128)S(1)} %get-tuple-element.10.motion, f32[3,128,128]{2,1,0:T(8,128)S(1)} %get-tuple-element.11.disp, ...), custom_call_target="tpu_custom_call" | custom-call | tf_op jit(solution)/shard_map/finish/pallas_call | solution.py:498

commit v5 on v4

--- a/solution.py
+++ b/solution.py
@@ -48,7 +48,7 @@
 def kernel(
     own_ref, node_ref, w_ref, nrm_ref, fluid_hbm, disp_hbm, vel_hbm,
     fo, motion_ref, disp_ref, base_ref, force,
-    xbuf, ybuf, zb, dbuf, vbuf,
+    xbuf, ybuf, pu, zb, dbuf, vbuf,
     onehot, rank, rankhot, reqb, req, asked, px,
     table, ohy, ohx, picked, rep, got, lookup, p0,
     loadb, outg, arrived, fb, colsend, collow, colhigh,
@@ -57,13 +57,15 @@
     span, chord = lax.axis_index("span"), lax.axis_index("chord")
     me = span * NC + chord
 
+    xs, zs = span // 4, lax.rem(span, 4)
     mine = span // 2
     slot_row = mine * 8 + chord + 64 * lax.rem(span, 2)
 
     loads = [
         pltpu.make_async_copy(disp_hbm, dbuf.at[:, pl.ds(8, 128)], in_sem.at[0]),
         pltpu.make_async_copy(vel_hbm, vbuf, in_sem.at[1]),
-        pltpu.make_async_copy(fluid_hbm, xbuf.at[:, pl.ds(3, CX)], in_sem.at[2]),
+        pltpu.make_async_copy(fluid_hbm.at[pl.ds(0, 2)], pu, in_sem.at[2]),
+        pltpu.make_async_copy(fluid_hbm.at[pl.ds(2, 2)], xbuf.at[pl.ds(2, 2), pl.ds(3, CX)], in_sem.at[5]),
         pltpu.make_async_copy(fluid_hbm.at[0], ybuf.at[0, :, pl.ds(8, CY)], in_sem.at[3]),
         pltpu.make_async_copy(fluid_hbm.at[2], ybuf.at[1, :, pl.ds(8, CY)], in_sem.at[4]),
     ]
@@ -72,31 +74,26 @@
 
     barrier = pltpu.get_barrier_semaphore()
 
-    def late_first(k, across):
-        a, b = k // 4, lax.rem(k, 4)
-        z = jnp.where(a < 2, 2 + a, 3 - a) if across == 4 else 1 - a
-        x = jnp.where(b == 0, 2, jnp.where(b == 3, 0, 2 * b - 1))
-        return x * across + z
-
-    def each_peer(act, backward=False):
+    def reach(k):
+        return jnp.where(k == 0, 2, jnp.where(k == 3, 0, 2 * k - 1))
+
+    def far_first(act):
         def one(k, carry):
-            s = late_first(NS - 1 - k if backward else k, 4)
-
-            @pl.when(s != span)
-            def _():
-                for c in range(NC):
-                    act(s, c)
-
+            act(lax.rem(xs + reach(k // 4), 4) * 4 + lax.rem(zs + reach(lax.rem(k, 4)), 4))
             return carry
 
-        lax.fori_loop(0, NS, one, 0)
+        lax.fori_loop(0, NS - 1, one, 0)
+
+    def greet(s):
         for c in range(NC):
-
-            @pl.when(c != chord)
-            def _():
-                act(span, c)
-
-    each_peer(lambda s, c: pl.semaphore_signal(barrier, 1, device_id=(s, c), device_id_type=MESH), True)
+            pl.semaphore_signal(barrier, 1, device_id=(s, c), device_id_type=MESH)
+
+    far_first(greet)
+    for c in range(NC):
+
+        @pl.when(c != chord)
+        def _():
+            pl.semaphore_signal(barrier, 1, device_id=(span, c), device_id_type=MESH)
 
     before = (iota((QW, QW), 0) < iota((QW, QW), 1)).astype(F32).astype(BF16)
     ones = jnp.ones((QW, QW), BF16)
@@ -146,26 +143,42 @@
     src, tgt = iota((NZ, NZ), 0), iota((NZ, NZ), 1)
     inner = stencil(src - tgt)
     ghost = jnp.where(src < 3, stencil(-(src + 1 + tgt)), 0.0)
-    for i, (f, tab) in enumerate(((0, inner + ghost), (3, inner - ghost))):
+    for i, tab in enumerate((inner + ghost, inner - ghost)):
         tab = tab.astype(BF16)
         tab = jnp.concatenate([tab, tab], axis=0)
         for b in range(4):
-            high, low = split(xbuf[f, 3 + 8 * b : 11 + 8 * b].reshape(256, NZ))
+            value = pu[0, 8 * b : 8 * b + 8] if i == 0 else xbuf[3, 3 + 8 * b : 11 + 8 * b]
+            high, low = split(value.reshape(256, NZ))
             zb[i, b * 256 : (b + 1) * 256, :] = dot(jnp.concatenate([high, low], axis=1), tab)
+
+    def blend(x, carry):
+        p, u = pu[0, x], pu[1, x]
+        xbuf[0, x + 3] = 0.5 * p + u
+        xbuf[1, x + 3] = 0.5 * u + p
+        return carry
+
+    lax.fori_loop(0, CX, blend, 0)
 
     pl.semaphore_wait(barrier, ND - 1)
 
     def row(ref, at):
         return ref.at[:, pl.ds(at, 1)]
 
+    def redirect(s, c):
+        own = (s == span) & (c == chord)
+        return own, jnp.where(own, lax.rem(chord + 1, NC), c)
+
     def exchange(src, dst, index, recv):
-        def send(s, c):
+        def send(s, c, row_at, to):
             pltpu.make_async_remote_copy(
-                row(src, s * NC + c), row(dst, slot_row), sent.at[index], recv.at[mine],
-                device_id=(s, c), device_id_type=MESH,
+                row(src, s * NC + c), row(dst, row_at), sent.at[index], recv.at[mine],
+                device_id=(s, to), device_id_type=MESH,
             ).start()
 
-        each_peer(send)
+        far_first(lambda s: [send(s, c, slot_row, c) for c in range(NC)])
+        for c in range(NC):
+            own, to = redirect(span, c)
+            send(span, c, jnp.where(own, ND, slot_row), to)
         dst[:, pl.ds(slot_row, 1), :] = src[:, pl.ds(me, 1), :]
 
     def some(src, dst, count, send_sem, recv_sem):
@@ -174,14 +187,10 @@
             device_id=(span, chord), device_id_type=MESH,
         )
 
-    def await_group(src, dst, index, recv, g):
-        @pl.when(g == mine)
-        def _():
-            some(src, dst, 15, sent.at[index], recv.at[g]).wait_recv()
-
-        @pl.when(g != mine)
-        def _():
-            some(src, dst, 16, sent.at[index], recv.at[g]).wait_recv()
+    def group_of(k):
+        dx = jnp.where(k < 2, 0, jnp.where(k < 4, 2, jnp.where(lax.rem(k, 2) == 0, 1, 3)))
+        dz = jnp.where(k < 2, k, jnp.where(k < 4, 3 - k, jnp.where(k < 6, 1, 0)))
+        return lax.rem(xs + dx, 4) * 2 + lax.rem(zs // 2 + dz, 2)
 
     exchange(req, asked, 0, ask_r)
 
@@ -190,10 +199,14 @@
     right = (span, lax.rem(chord + 1, NC))
     left = (span, lax.rem(chord + NC - 1, NC))
     moves = [
-        (xbuf.at[:, pl.ds(CX, 3)], xbuf.at[:, pl.ds(0, 3)], up),
-        (xbuf.at[:, pl.ds(3, 3)], xbuf.at[:, pl.ds(CX + 3, 3)], down),
-        (ybuf.at[:, :, pl.ds(CY + 5, 3)], ybuf.at[:, :, pl.ds(5, 3)], right),
-        (ybuf.at[:, :, pl.ds(8, 3)], ybuf.at[:, :, pl.ds(CY + 8, 3)], left),
+        (xbuf.at[0, pl.ds(CX, 3)], xbuf.at[0, pl.ds(0, 3)], up),
+        (xbuf.at[0, pl.ds(3, 3)], xbuf.at[0, pl.ds(CX + 3, 3)], down),
+        (ybuf.at[1, :, pl.ds(CY + 5, 3)], ybuf.at[1, :, pl.ds(5, 3)], right),
+        (ybuf.at[1, :, pl.ds(8, 3)], ybuf.at[1, :, pl.ds(CY + 8, 3)], left),
+        (xbuf.at[pl.ds(1, 3), pl.ds(CX, 3)], xbuf.at[pl.ds(1, 3), pl.ds(0, 3)], up),
+        (xbuf.at[pl.ds(1, 3), pl.ds(3, 3)], xbuf.at[pl.ds(1, 3), pl.ds(CX + 3, 3)], down),
+        (ybuf.at[0, :, pl.ds(CY + 5, 3)], ybuf.at[0, :, pl.ds(5, 3)], right),
+        (ybuf.at[0, :, pl.ds(8, 3)], ybuf.at[0, :, pl.ds(CY + 8, 3)], left),
         (dbuf.at[:, pl.ds(135, 1)], dbuf.at[:, pl.ds(7, 1)], up),
         (dbuf.at[:, pl.ds(8, 1)], dbuf.at[:, pl.ds(136, 1)], down),
         (colsend.at[1], collow, right),
@@ -203,7 +216,7 @@
         pltpu.make_async_remote_copy(a, b, halo_s.at[i], halo_r.at[i], device_id=to, device_id_type=MESH)
         for i, (a, b, to) in enumerate(moves)
     ]
-    for h in halos:
+    for h in halos[:4]:
         h.start()
 
     lane8 = iota((8, 128), 1)
@@ -226,19 +239,15 @@
         back = jnp.where(lane8 < 64, pltpu.roll(low, 64, 1), high)
         return front, back
 
-    def pick(k, carry):
-        g = late_first(k, 2)
-        await_group(req, asked, 0, ask_r, g)
-        rows = pl.ds(pl.multiple_of(g * 8, 8), 8)
-        xs, ys = halves(asked, 0, g)
-        px[rows, :] = xs
-        group = [pl.ds(pl.multiple_of((g * 4 + t) * QW, QW), QW) for t in range(4)]
+    def pick(k, g):
+        xs_, ys_ = halves(asked, 0, g)
+        px[k * 8 : (k + 1) * 8, :] = xs_
         for t in range(4):
-            yrow = jnp.concatenate([ys[2 * t : 2 * t + 1], ys[2 * t + 1 : 2 * t + 2]], axis=1)
-            ohy[:, group[t]] = hot_rows(low_y, yrow, 256)
+            yrow = jnp.concatenate([ys_[2 * t : 2 * t + 1], ys_[2 * t + 1 : 2 * t + 2]], axis=1)
+            ohy[:, (4 * k + t) * QW : (4 * k + t + 1) * QW] = hot_rows(low_y, yrow, 256)
         for t in range(4):
-            xrow = jnp.concatenate([xs[2 * t : 2 * t + 1], xs[2 * t + 1 : 2 * t + 2]], axis=1)
-            hot = ohy[:, group[t]]
+            xrow = jnp.concatenate([xs_[2 * t : 2 * t + 1], xs_[2 * t + 1 : 2 * t + 2]], axis=1)
+            hot = ohy[:, (4 * k + t) * QW : (4 * k + t + 1) * QW]
             out = dot(table[...], jnp.concatenate([hot, hot], axis=0))
             sums = [jnp.zeros((8, QW), F32) for _ in range(6)]
             for i in range(8):
@@ -248,95 +257,92 @@
                     sums[c] = sums[c] + jnp.where(mask, out[at : at + 8], 0.0)
             for c in range(6):
                 line = jnp.sum(sums[c], axis=0, keepdims=True)
-                picked[c, 2 * t : 2 * t + 1, :] = line[:, 0:128]
-                picked[c, 2 * t + 1 : 2 * t + 2, :] = line[:, 128:256]
-        high_rows = pl.ds(pl.multiple_of(g * 8 + 64, 8), 8)
+                picked[k % 2, c, 2 * t : 2 * t + 1, :] = line[:, 0:128]
+                picked[k % 2, c, 2 * t + 1 : 2 * t + 2, :] = line[:, 128:256]
         for j in range(3):
-            even, odd = picked[2 * j], picked[2 * j + 1]
-            rep[j, rows, :] = jnp.where(lane8 < 64, even, pltpu.roll(odd, 64, 1))
-            rep[j, high_rows, :] = jnp.where(lane8 < 64, pltpu.roll(even, 64, 1), odd)
-
-        def reply(half, c):
-            pltpu.make_async_remote_copy(
-                row(rep, g * 8 + c + 64 * half), row(got, me), sent.at[1], reply_r,
-                device_id=(2 * g + half, c), device_id_type=MESH,
-            ).start()
-
-        @pl.when(g != mine)
+            even, odd = picked[k % 2, 2 * j], picked[k % 2, 2 * j + 1]
+            rep[j, k * 16 : k * 16 + 8, :] = jnp.where(lane8 < 64, even, pltpu.roll(odd, 64, 1))
+            rep[j, k * 16 + 8 : k * 16 + 16, :] = jnp.where(lane8 < 64, pltpu.roll(even, 64, 1), odd)
+
+    def reply(k, g):
+        for half in range(2):
+            for c in range(NC):
+                to, at = c, me
+                if k == 0:
+                    own, to = redirect(2 * g + half, c)
+                    at = jnp.where(own, ND, me)
+                pltpu.make_async_remote_copy(
+                    row(rep, k * 16 + 8 * half + c), row(got, at), sent.at[1], reply_r,
+                    device_id=(2 * g + half, to), device_id_type=MESH,
+                ).start()
+
+    order = [group_of(k) for k in range(8)]
+    for pair in range(4):
+        for k in (2 * pair, 2 * pair + 1):
+            some(req, asked, 16, sent.at[0], ask_r.at[order[k]]).wait_recv()
+        if pair:
+            reply(2 * pair - 2, order[2 * pair - 2])
+            reply(2 * pair - 1, order[2 * pair - 1])
+        pick(2 * pair, order[2 * pair])
+        pick(2 * pair + 1, order[2 * pair + 1])
+    reply(6, order[6])
+    reply(7, order[7])
+    got[:, pl.ds(me, 1), :] = rep[:, pl.ds(8 * lax.rem(span, 2) + chord, 1), :]
+
+    for h in halos[4:]:
+        h.start()
+
+    def arrive(group, fields, yfield):
+        for h in group:
+            h.wait_recv()
+
+        @pl.when(span == 0)
         def _():
-            for half in range(2):
-                for c in range(NC):
-                    reply(half, c)
-
-        @pl.when(g == mine)
+            xbuf[fields, 0:3] = jnp.zeros((fields.stop - fields.start, 3, CY, NZ), F32)
+
+        @pl.when(span == NS - 1)
         def _():
-            for half in range(2):
-                for c in range(NC):
-
-                    @pl.when((2 * g + half != span) | (c != chord))
-                    def _():
-                        reply(half, c)
-
+            xbuf[fields, CX + 3 : CX + 6] = jnp.zeros((fields.stop - fields.start, 3, CY, NZ), F32)
+
+        @pl.when(chord == 0)
+        def _():
+            ybuf[yfield, :, 5:8, :] = jnp.zeros((CX, 3, NZ), F32)
+
+        @pl.when(chord == NC - 1)
+        def _():
+            ybuf[yfield, :, CY + 8 : CY + 11, :] = jnp.zeros((CX, 3, NZ), F32)
+
+    def dx(f, x):
+        return diff(*[xbuf[f, x + 3 + o] for o in (3, 2, 1, -1, -2, -3)])
+
+    def dy(f, x):
+        return diff(*[ybuf[f, x, 8 + o : 8 + CY + o, :] for o in (3, 2, 1, -1, -2, -3)])
+
+    def zrows(x):
+        return pl.ds(pl.multiple_of(x * CY, CY), CY)
+
+    def plane_p(x, carry):
+        fo[0, x] = pu[0, x] - SCALE * (dx(0, x) + dy(1, x) + zb[1, zrows(x), :])
         return carry
 
-    lax.fori_loop(0, 8, pick, 0)
-    got[:, pl.ds(me, 1), :] = rep[:, pl.ds(slot_row, 1), :]
-
-    for h in halos:
-        h.wait_recv()
-
-    @pl.when(span == 0)
-    def _():
-        xbuf[:, 0:3] = jnp.zeros((4, 3, CY, NZ), F32)
-        dbuf[:, 7:8, :] = jnp.zeros((3, 1, 128), F32)
-
-    @pl.when(span == NS - 1)
-    def _():
-        xbuf[:, CX + 3 : CX + 6] = jnp.zeros((4, 3, CY, NZ), F32)
-        dbuf[:, 136:137, :] = jnp.zeros((3, 1, 128), F32)
-
-    @pl.when(chord == 0)
-    def _():
-        ybuf[:, :, 5:8, :] = jnp.zeros((2, CX, 3, NZ), F32)
-        collow[...] = jnp.zeros((8, 128), F32)
-
-    @pl.when(chord == NC - 1)
-    def _():
-        ybuf[:, :, CY + 8 : CY + 11, :] = jnp.zeros((2, CX, 3, NZ), F32)
-        colhigh[...] = jnp.zeros((8, 128), F32)
-
-    def plane(x, carry):
-        def dx(f):
-            return diff(*[xbuf[f, x + 3 + o] for o in (3, 2, 1, -1, -2, -3)])
-
-        def dy(f):
-            return diff(*[ybuf[f, x, 8 + o : 8 + CY + o, :] for o in (3, 2, 1, -1, -2, -3)])
-
-        zrows = pl.ds(pl.multiple_of(x * CY, CY), CY)
-        dp, du = dx(0), dx(1)
-        fo[0, x] = xbuf[0, x + 3] - SCALE * (0.5 * dp + du + dy(1) + zb[1, zrows, :])
-        fo[1, x] = xbuf[1, x + 3] - SCALE * (0.5 * du + dp)
-        fo[2, x] = xbuf[2, x + 3] - SCALE * (0.5 * dx(2) + dy(0))
-        fo[3, x] = xbuf[3, x + 3] - SCALE * (0.5 * dx(3) + zb[0, zrows, :])
-        return carry
-
-    lax.fori_loop(0, CX, plane, 0)
+    arrive(halos[:4], slice(0, 1), 1)
+    lax.fori_loop(0, CX, plane_p, 0)
     for b in range(8):
         turned = fo[0, 4 * b : 4 * b + 4].reshape(128, NZ).T
         p0[0:1, b * 128 : (b + 1) * 128] = turned[0:1, :]
 
     def columns(g, carry):
         rows = pl.ds(pl.multiple_of(g * 8, 8), 8)
-        xs = px[rows, :]
+        places = px[rows, :]
         for t in range(8):
-            ohx[:, pl.ds(pl.multiple_of((g * 8 + t) * 128, 128), 128)] = hot_rows(low_x, xs[t : t + 1], 64)
+            ohx[:, pl.ds(pl.multiple_of((g * 8 + t) * 128, 128), 128)] = hot_rows(low_x, places[t : t + 1], 64)
         return carry
 
     lax.fori_loop(0, 8, columns, 0)
 
-    some(rep, got, ND - 1, sent.at[1], reply_r).wait_recv()
+    some(rep, got, ND, sent.at[1], reply_r).wait_recv()
     for j in range(3):
-        high, low = split(got[j].T)
+        high, low = split(got[j, 0:ND].T)
         for c in range(2):
             for t in range(4):
                 at = t * 96 + (2 * j + c) * 16
@@ -345,7 +351,7 @@
 
     sub8i = iota((8, QW), 0)
 
-    def interp(q, carry):
+    def interp(q):
         cols = pl.ds(pl.multiple_of(q * QW, QW), QW)
         totals = [jnp.zeros((8, QW), F32) for _ in range(6)]
         for k in range(K):
@@ -363,9 +369,13 @@
                 totals[c] = totals[c] + weight * sums[c]
         for c in range(6):
             motion_ref[c : c + 1, cols] = jnp.sum(totals[c], axis=0, keepdims=True)
+
+    def interp_two(i, carry):
+        interp(2 * i)
+        interp(2 * i + 1)
         return carry
 
-    lax.fori_loop(0, PTS // QW, interp, 0)
+    lax.fori_loop(0, PTS // QW // 2, interp_two, 0)
 
     pressure = p0[0:1, :] + (SCALE * 74.0) * motion_ref[5:6, :]
     both = jnp.zeros((ND, 384), F32)
@@ -383,6 +393,32 @@
     outg[1] = both[:, 256:384] + pltpu.roll(both[:, 256:384], 64, 1)
     exchange(outg, arrived, 2, load_r)
 
+    def plane_v(x, carry):
+        fo[1, x] = pu[1, x] - SCALE * dx(1, x)
+        fo[2, x] = xbuf[2, x + 3] - SCALE * (0.5 * dx(2, x) + dy(0, x))
+        fo[3, x] = xbuf[3, x + 3] - SCALE * (0.5 * dx(3, x) + zb[0, zrows(x), :])
+        return carry
+
+    arrive(halos[4:], slice(1, 4), 0)
+
+    @pl.when(span == 0)
+    def _():
+        dbuf[:, 7:8, :] = jnp.zeros((3, 1, 128), F32)
+
+    @pl.when(span == NS - 1)
+    def _():
+        dbuf[:, 136:137, :] = jnp.zeros((3, 1, 128), F32)
+
+    @pl.when(chord == 0)
+    def _():
+        collow[...] = jnp.zeros((8, 128), F32)
+
+    @pl.when(chord == NC - 1)
+    def _():
+        colhigh[...] = jnp.zeros((8, 128), F32)
+
+    lax.fori_loop(0, CX, plane_v, 0)
+
     zlane = iota((128, NZ), 1)
     reach = jnp.where(zlane == 0, 74.0 * SCALE, jnp.where(zlane == 1, -16.0 * SCALE, jnp.where(zlane == 2, 2.0 * SCALE, 0.0)))
     for b in range(8):
@@ -402,15 +438,16 @@
         disp_ref[c] = mid
 
     def collect(k, carry):
-        g = late_first(k, 2)
-        await_group(outg, arrived, 2, load_r, g)
-        cols = pl.ds(pl.multiple_of(g * 1024, 1024), 1024)
+        k = jnp.where(k < 2, k, jnp.where(k < 4, k + 4, jnp.where(k < 6, k, 9 - k)))
+        g = group_of(k)
+        some(outg, arrived, 16, sent.at[2], load_r.at[g]).wait_recv()
+        cols = pl.ds(pl.multiple_of(k * 1024, 1024), 1024)
         values = halves(arrived, 0, g) + halves(arrived, 1, g)[0:1]
         for c in range(3):
             high = values[c].astype(BF16).astype(F32)
             for half, value in enumerate((high, values[c] - high)):
                 for t in range(8):
-                    hot = ohx[:, pl.ds(pl.multiple_of((g * 8 + t) * 128, 128), 128)]
+                    hot = ohx[:, pl.ds(pl.multiple_of((k * 8 + t) * 128, 128), 128)]
                     at = (half * 3 + c) * 64
                     fb[at : at + 64, t * 128 : (t + 1) * 128] = hot * tall(value[t : t + 1], 64)
         force[...] += dot_nt(fb[...], ohy[:, cols])
@@ -420,7 +457,7 @@
     for h in halos:
         h.wait_send()
     for index, (src, dst) in enumerate(((req, asked), (rep, got), (outg, arrived))):
-        some(src, dst, ND - 1, sent.at[index], reply_r).wait_send()
+        some(src, dst, ND, sent.at[index], reply_r).wait_send()
 
 
 def finish(fo, motion, disp, base, force, fo_out, motion_out, disp_out, vel_out, disp_new, vel_new, sems):
@@ -449,6 +486,7 @@
     scratch = [
         vm((4, CX + 6, CY, NZ), F32),
         vm((2, CX, CY + 16, NZ), F32),
+        vm((2, CX, CY, NZ), F32),
         vm((2, PTS, NZ), F32),
         vm((3, 144, 128), F32),
         vm((3, 128, 128), F32),
@@ -457,26 +495,26 @@
         vm((CAP, ENT), BF16),
         vm((128, ENT), BF16),
         vm((1, ND, 128), F32),
-        vm((1, ND, 128), F32),
+        vm((1, ND + 8, 128), F32),
         vm((CAP, 128), F32),
         vm((384, 512), BF16),
         vm((256, SLOTS), BF16),
         vm((64, SLOTS), BF16),
-        vm((6, 8, 128), F32),
+        vm((2, 6, 8, 128), F32),
         vm((3, ND, 128), F32),
-        vm((3, ND, 128), F32),
+        vm((3, ND + 8, 128), F32),
         vm((384, 256), BF16),
         vm((8, PTS), F32),
         vm((384, ENT), BF16),
         vm((2, ND, 128), F32),
-        vm((2, ND, 128), F32),
+        vm((2, ND + 8, 128), F32),
         vm((384, 1024), BF16),
         vm((2, 8, 128), F32),
         vm((8, 128), F32),
         vm((8, 128), F32),
-        dma((5,)),
-        dma((8,)),
-        dma((8,)),
+        dma((6,)),
+        dma((12,)),
+        dma((12,)),
         dma((3,)),
         dma((8,)),
         dma(()),

time: 41.6 us -> 40.5 us (0.974)
  Pallas kernels: 40.7 us -> 39.6 us
    pallas_call x1, Pallas kernels: 39.2 us -> 38.1 us  [body(): pl.pallas_call(kernel, name='coupling', out_shape=tuple((vm(shape, F32) f...]
where the time goes in v5:
time: 40.5 us; the launch traced here: 40.2 us
  Pallas kernels  39.6 us (98%)
  between operations  0.64 us (2%)
    pallas_call x1, Pallas kernels, body(): pl.pallas_call(kernel, name='coupling', out_shape=tuple((vm(shape, F32) f...  38.1 us
    pallas_call x1, Pallas kernels, body(): pl.pallas_call(finish, name='finish', out_shape=tuple((jax.ShapeDtypeStru...  1.51 us

profile of v5, /device:TPU:1, one launch (start us, length us, event | category | flops | bytes accessed | tf_op | source)
XLA Modules:
  0.0 40.2 jit_solution(852252871624632848)
XLA Ops:
  0.6 38.1 %coupling.1 = (f32[4,32,32,128]{3,2,1,0:T(8,128)S(1)}, f32[6,1024]{1,0:T(8,128)S(1)}, f32[3,128,128]{2,1,0:T(8,128)S(1)}, f32[3,128,128]{2,1,0:T(8,128)S(1)}, f32[384,256]{1,0:T(8,128)S(1)}) custom-call(s32[4,1024]{1,0:T(4,128)} %bitcast.3, s32[4,1024]{1,0:T(4,128)} %bitcast.4, f32[4,1024]{1,0:T(4,128)} %bitcast.5, f32[3,1024]{1,0:T(4,128)} %nrm_ref.1, ...), custom_call_target="tpu_custom_call" | custom-call | tf_op jit(solution)/shard_map/coupling/pallas_call | solution.py:525
  38.7 1.5 %finish.1 = (f32[4,32,32,128]{3,2,1,0:T(8,128)}, f32[6,1024]{1,0:T(8,128)}, f32[3,128,128]{2,1,0:T(8,128)}, f32[3,128,128]{2,1,0:T(8,128)}) custom-call(f32[4,32,32,128]{3,2,1,0:T(8,128)S(1)} %get-tuple-element.9.fo, f32[6,1024]{1,0:T(8,128)S(1)} %get-tuple-element.10.motion, f32[3,128,128]{2,1,0:T(8,128)S(1)} %get-tuple-element.11.disp, ...), custom_call_target="tpu_custom_call" | custom-call | tf_op jit(solution)/shard_map/finish/pallas_call | solution.py:536

commit v6 on v5

--- a/solution.py
+++ b/solution.py
@@ -45,12 +45,35 @@
     return jnp.where(distance > 0, value, -value)
 
 
+def tall(line, rows):
+    wide = jnp.broadcast_to(line, (16, line.shape[1])).astype(BF16)
+    return jnp.concatenate([wide] * (rows // 16), axis=0)
+
+
+EARLY, LATE = ((0, 1),), (6, 7, 4, 5, 3, 2)
+
+
+def weigh(part, ready, ohx, ohy, fb):
+    for i, k in enumerate(part):
+        for c in range(3):
+            high = ready[i][c].astype(BF16).astype(F32)
+            for half, value in enumerate((high, ready[i][c] - high)):
+                for t in range(8):
+                    hot = ohx[:, (k * 8 + t) * 128 : (k * 8 + t + 1) * 128]
+                    at = (half * 3 + c) * 64
+                    fb[at : at + 64, i * 1024 + t * 128 : i * 1024 + (t + 1) * 128] = hot * tall(value[t : t + 1], 64)
+    total = jnp.zeros((384, 256), F32)
+    for i, k in enumerate(part):
+        total = total + dot_nt(fb[:, i * 1024 : (i + 1) * 1024], ohy[:, k * 1024 : (k + 1) * 1024])
+    return total
+
+
 def kernel(
     own_ref, node_ref, w_ref, nrm_ref, fluid_hbm, disp_hbm, vel_hbm,
-    fo, motion_ref, disp_ref, base_ref, force,
+    fo, motion_ref, disp_ref, base_ref, force, late, ohx, ohy,
     xbuf, ybuf, pu, zb, dbuf, vbuf,
     onehot, rank, rankhot, reqb, req, asked, px,
-    table, ohy, ohx, picked, rep, got, lookup, p0,
+    table, picked, rep, got, lookup, p0,
     loadb, outg, arrived, fb, colsend, collow, colhigh,
     in_sem, halo_s, halo_r, sent, ask_r, reply_r, load_r,
 ):
@@ -138,7 +161,6 @@
         turned = dbuf[c, 8:136, :].T
         colsend[0, c : c + 1, :] = turned[0:1, :]
         colsend[1, c : c + 1, :] = turned[127:128, :]
-    force[...] = jnp.zeros((384, 256), F32)
 
     src, tgt = iota((NZ, NZ), 0), iota((NZ, NZ), 1)
     inner = stencil(src - tgt)
@@ -216,7 +238,7 @@
         pltpu.make_async_remote_copy(a, b, halo_s.at[i], halo_r.at[i], device_id=to, device_id_type=MESH)
         for i, (a, b, to) in enumerate(moves)
     ]
-    for h in halos[:4]:
+    for h in halos:
         h.start()
 
     lane8 = iota((8, 128), 1)
@@ -224,10 +246,6 @@
     low_y = iota((256, QW), 0).astype(F32).astype(BF16)
     low_x = iota((64, 128), 0).astype(F32).astype(BF16)
     one, zero = jnp.ones((), BF16), jnp.zeros((), BF16)
-
-    def tall(line, rows):
-        wide = jnp.broadcast_to(line, (16, line.shape[1])).astype(BF16)
-        return jnp.concatenate([wide] * (rows // 16), axis=0)
 
     def hot_rows(numbers, line, rows):
         return jnp.where(numbers == tall(line, rows), one, zero)
@@ -280,17 +298,11 @@
     for pair in range(4):
         for k in (2 * pair, 2 * pair + 1):
             some(req, asked, 16, sent.at[0], ask_r.at[order[k]]).wait_recv()
-        if pair:
-            reply(2 * pair - 2, order[2 * pair - 2])
-            reply(2 * pair - 1, order[2 * pair - 1])
         pick(2 * pair, order[2 * pair])
         pick(2 * pair + 1, order[2 * pair + 1])
-    reply(6, order[6])
-    reply(7, order[7])
+        reply(2 * pair, order[2 * pair])
+        reply(2 * pair + 1, order[2 * pair + 1])
     got[:, pl.ds(me, 1), :] = rep[:, pl.ds(8 * lax.rem(span, 2) + chord, 1), :]
-
-    for h in halos[4:]:
-        h.start()
 
     def arrive(group, fields, yfield):
         for h in group:
@@ -339,6 +351,43 @@
         return carry
 
     lax.fori_loop(0, 8, columns, 0)
+
+    def plane_v(x, carry):
+        fo[1, x] = pu[1, x] - SCALE * dx(1, x)
+        fo[2, x] = xbuf[2, x + 3] - SCALE * (0.5 * dx(2, x) + dy(0, x))
+        fo[3, x] = xbuf[3, x + 3] - SCALE * (0.5 * dx(3, x) + zb[0, zrows(x), :])
+        return carry
+
+    arrive(halos[4:], slice(1, 4), 0)
+
+    @pl.when(span == 0)
+    def _():
+        dbuf[:, 7:8, :] = jnp.zeros((3, 1, 128), F32)
+
+    @pl.when(span == NS - 1)
+    def _():
+        dbuf[:, 136:137, :] = jnp.zeros((3, 1, 128), F32)
+
+    @pl.when(chord == 0)
+    def _():
+        collow[...] = jnp.zeros((8, 128), F32)
+
+    @pl.when(chord == NC - 1)
+    def _():
+        colhigh[...] = jnp.zeros((8, 128), F32)
+
+    lax.fori_loop(0, CX, plane_v, 0)
+
+    lane128 = iota((128, 128), 1)
+    low_t, high_t = collow[...].T, colhigh[...].T
+    for c in range(3):
+        mid = dbuf[c, 8:136, :]
+        west = jnp.where(lane128 == 0, low_t[:, c : c + 1], pltpu.roll(mid, 1, 1))
+        east = jnp.where(lane128 == 127, high_t[:, c : c + 1], pltpu.roll(mid, 127, 1))
+        lap = dbuf[c, 9:137, :] + dbuf[c, 7:135, :] + east + west - 4.0 * mid
+        vel = vbuf[c]
+        base_ref[c] = vel + 0.3 * (0.5 * lap - 0.2 * vel)
+        disp_ref[c] = mid
 
     some(rep, got, ND, sent.at[1], reply_r).wait_recv()
     for j in range(3):
@@ -393,32 +442,6 @@
     outg[1] = both[:, 256:384] + pltpu.roll(both[:, 256:384], 64, 1)
     exchange(outg, arrived, 2, load_r)
 
-    def plane_v(x, carry):
-        fo[1, x] = pu[1, x] - SCALE * dx(1, x)
-        fo[2, x] = xbuf[2, x + 3] - SCALE * (0.5 * dx(2, x) + dy(0, x))
-        fo[3, x] = xbuf[3, x + 3] - SCALE * (0.5 * dx(3, x) + zb[0, zrows(x), :])
-        return carry
-
-    arrive(halos[4:], slice(1, 4), 0)
-
-    @pl.when(span == 0)
-    def _():
-        dbuf[:, 7:8, :] = jnp.zeros((3, 1, 128), F32)
-
-    @pl.when(span == NS - 1)
-    def _():
-        dbuf[:, 136:137, :] = jnp.zeros((3, 1, 128), F32)
-
-    @pl.when(chord == 0)
-    def _():
-        collow[...] = jnp.zeros((8, 128), F32)
-
-    @pl.when(chord == NC - 1)
-    def _():
-        colhigh[...] = jnp.zeros((8, 128), F32)
-
-    lax.fori_loop(0, CX, plane_v, 0)
-
     zlane = iota((128, NZ), 1)
     reach = jnp.where(zlane == 0, 74.0 * SCALE, jnp.where(zlane == 1, -16.0 * SCALE, jnp.where(zlane == 2, 2.0 * SCALE, 0.0)))
     for b in range(8):
@@ -426,47 +449,37 @@
         fix = (turned[:, 0:1] * reach).reshape(4, CY, NZ)
         fo[0, 4 * b : 4 * b + 4] = fo[0, 4 * b : 4 * b + 4] + fix
 
-    lane128 = iota((128, 128), 1)
-    low_t, high_t = collow[...].T, colhigh[...].T
-    for c in range(3):
-        mid = dbuf[c, 8:136, :]
-        west = jnp.where(lane128 == 0, low_t[:, c : c + 1], pltpu.roll(mid, 1, 1))
-        east = jnp.where(lane128 == 127, high_t[:, c : c + 1], pltpu.roll(mid, 127, 1))
-        lap = dbuf[c, 9:137, :] + dbuf[c, 7:135, :] + east + west - 4.0 * mid
-        vel = vbuf[c]
-        base_ref[c] = vel + 0.3 * (0.5 * lap - 0.2 * vel)
-        disp_ref[c] = mid
-
-    def collect(k, carry):
-        k = jnp.where(k < 2, k, jnp.where(k < 4, k + 4, jnp.where(k < 6, k, 9 - k)))
-        g = group_of(k)
+    def loads_of(k):
+        g = order[k]
         some(outg, arrived, 16, sent.at[2], load_r.at[g]).wait_recv()
-        cols = pl.ds(pl.multiple_of(k * 1024, 1024), 1024)
-        values = halves(arrived, 0, g) + halves(arrived, 1, g)[0:1]
-        for c in range(3):
-            high = values[c].astype(BF16).astype(F32)
-            for half, value in enumerate((high, values[c] - high)):
-                for t in range(8):
-                    hot = ohx[:, pl.ds(pl.multiple_of((k * 8 + t) * 128, 128), 128)]
-                    at = (half * 3 + c) * 64
-                    fb[at : at + 64, t * 128 : (t + 1) * 128] = hot * tall(value[t : t + 1], 64)
-        force[...] += dot_nt(fb[...], ohy[:, cols])
-        return carry
-
-    lax.fori_loop(0, 8, collect, 0)
+        return halves(arrived, 0, g) + halves(arrived, 1, g)[0:1]
+
+    for index, part in enumerate(EARLY):
+        ready = [loads_of(k) for k in part]
+        total = weigh(part, ready, ohx, ohy, fb)
+        force[...] = total if index == 0 else force[...] + total
+    for i, k in enumerate(LATE):
+        for c, value in enumerate(loads_of(k)):
+            late[3 * i + c] = value
+
     for h in halos:
         h.wait_send()
     for index, (src, dst) in enumerate(((req, asked), (rep, got), (outg, arrived))):
         some(src, dst, ND, sent.at[index], reply_r).wait_send()
 
 
-def finish(fo, motion, disp, base, force, fo_out, motion_out, disp_out, vel_out, disp_new, vel_new, sems):
+def finish(
+    fo, motion, disp, base, force, late, ohx, ohy,
+    fo_out, motion_out, disp_out, vel_out,
+    disp_new, vel_new, fb, sems,
+):
     pairs = [(fo.at[i], fo_out.at[i]) for i in range(4)] + [(motion, motion_out), (disp_new, disp_out), (vel_new, vel_out)]
     copies = [pltpu.make_async_copy(a, b, sems.at[i]) for i, (a, b) in enumerate(pairs)]
     for c in copies[:5]:
         c.start()
+    sums = force[...] + weigh(LATE, [[late[3 * i + c] for c in range(3)] for i in range(len(LATE))], ohx, ohy, fb)
     for c in range(3):
-        total = force[c * 64 : (c + 1) * 64, :] + force[192 + c * 64 : 192 + (c + 1) * 64, :]
+        total = sums[c * 64 : (c + 1) * 64, :] + sums[192 + c * 64 : 192 + (c + 1) * 64, :]
         for odd in range(2):
             rows = pl.ds(odd, 64, stride=2)
             vel = base[c, rows, :] + 0.3 * total[:, odd * 128 : (odd + 1) * 128]
@@ -498,8 +511,6 @@
         vm((1, ND + 8, 128), F32),
         vm((CAP, 128), F32),
         vm((384, 512), BF16),
-        vm((256, SLOTS), BF16),
-        vm((64, SLOTS), BF16),
         vm((2, 6, 8, 128), F32),
         vm((3, ND, 128), F32),
         vm((3, ND + 8, 128), F32),
@@ -508,7 +519,7 @@
         vm((384, ENT), BF16),
         vm((2, ND, 128), F32),
         vm((2, ND + 8, 128), F32),
-        vm((384, 1024), BF16),
+        vm((384, 2048), BF16),
         vm((2, 8, 128), F32),
         vm((8, 128), F32),
         vm((8, 128), F32),
@@ -521,26 +532,27 @@
         dma((8,)),
     ]
     shapes = (fluid.shape, (6, PTS), disp.shape, vel.shape)
-    kept = shapes + ((384, 256),)
+    kept = [vm(shape, F32) for shape in shapes + ((384, 256), (3 * len(LATE), 8, 128))]
+    kept += [vm((64, SLOTS), BF16), vm((256, SLOTS), BF16)]
     done = pl.pallas_call(
         kernel,
         name="coupling",
-        out_shape=tuple(vm(shape, F32) for shape in kept),
+        out_shape=tuple(kept),
         in_specs=[small] * 4 + [big] * 3,
-        out_specs=(small,) * 5,
+        out_specs=(small,) * 8,
         scratch_shapes=scratch,
         compiler_params=pltpu.CompilerParams(
-            collective_id=0, has_side_effects=True, vmem_limit_bytes=64_000_000
+            collective_id=0, has_side_effects=True, vmem_limit_bytes=58_400_000
         ),
     )(owners.T, nodes.T, weights.T, normals, fluid, disp, vel)
     return pl.pallas_call(
         finish,
         name="finish",
         out_shape=tuple(jax.ShapeDtypeStruct(shape, F32) for shape in shapes),
-        in_specs=[small] * 5,
+        in_specs=[small] * 8,
         out_specs=(big,) * 4,
-        scratch_shapes=[vm(disp.shape, F32), vm(vel.shape, F32), dma((7,))],
-        compiler_params=pltpu.CompilerParams(vmem_limit_bytes=1024 * 1024),
+        scratch_shapes=[vm(disp.shape, F32), vm(vel.shape, F32), vm((384, 1024 * len(LATE)), BF16), dma((7,))],
+        compiler_params=pltpu.CompilerParams(vmem_limit_bytes=6 * 1024 * 1024),
     )(*[pltpu.with_memory_space_constraint(part, pltpu.VMEM) for part in done])
 
 

time: 40.5 us -> 39.4 us (0.973)
  Pallas kernels: 39.6 us -> 38.5 us
    pallas_call x1, Pallas kernels: 38.1 us -> 36.2 us  [body(): pl.pallas_call(kernel, name='coupling', out_shape=tuple(kept), in_specs=[...]
    pallas_call x1, Pallas kernels: 1.51 us -> 2.29 us  [body(): pl.pallas_call(finish, name='finish', out_shape=tuple((jax.ShapeDtypeStru...]
where the time goes in v6:
time: 39.4 us; the launch traced here: 39.2 us
  Pallas kernels  38.5 us (98%)
  between operations  0.64 us (2%)
    pallas_call x1, Pallas kernels, body(): pl.pallas_call(kernel, name='coupling', out_shape=tuple(kept), in_specs=[...  36.2 us
    pallas_call x1, Pallas kernels, body(): pl.pallas_call(finish, name='finish', out_shape=tuple((jax.ShapeDtypeStru...  2.29 us

profile of v6, /device:TPU:1, one launch (start us, length us, event | category | flops | bytes accessed | tf_op | source)
XLA Modules:
  0.0 39.2 jit_solution(16603681142757090036)
XLA Ops:
  0.6 36.2 %coupling.1 = (f32[4,32,32,128]{3,2,1,0:T(8,128)S(1)}, f32[6,1024]{1,0:T(8,128)S(1)}, f32[3,128,128]{2,1,0:T(8,128)S(1)}, f32[3,128,128]{2,1,0:T(8,128)S(1)}, f3...) custom-call(s32[4,1024]{1,0:T(4,128)} %bitcast.3, ...), custom_call_target="tpu_custom_call" | custom-call | tf_op jit(solution)/shard_map/coupling/pallas_call | solution.py:537
  36.9 2.3 %finish.1 = (f32[4,32,32,128]{3,2,1,0:T(8,128)}, f32[6,1024]{1,0:T(8,128)}, f32[3,128,128]{2,1,0:T(8,128)}, f32[3,128,128]{2,1,0:T(8,128)}) custom-call(f32[4,32,32,128]{3,2,1,0:T(8,128)S(1)} %get-tuple-element.12.fo, f32[6,1024]{1,0:T(8,128)S(1)} %get-tuple-element.13.motion, f32[3,128,128]{2,1,0:T(8,128)S(1)} %get-tuple-element.14.disp, ...), custom_call_target="tpu_custom_call" | custom-call | tf_op jit(solution)/shard_map/finish/pallas_call | solution.py:548
